TPU v7x, 32 devices: a whole 2x2x4 slice. The times are simulated.
32 devices in a mesh: row: 4 (over y, core), col: 8 (over z, x).
Axes of the slice: x: 2, y: 2, z: 4, core: 2. Of those that a mesh axis runs over, the one named last changes fastest.
Arguments:
- b_tensor: bfloat16 [128, 1024, 1024], P('col', 'row'), may hold values from -6 to 6
- occ_green: bfloat16 [1024, 1024], P(('row', 'col')), may hold values from -0.1875 to 0.1875
- virt_green: bfloat16 [1024, 1024], P(('row', 'col')), may hold values from -0.1875 to 0.1875
- b_mask: int32 [1, 8, 8], replicated, may hold values 0 or 1
- occ_mask: int32 [8, 8], replicated, may hold values 0 or 1
- virt_mask: int32 [8, 8], replicated, may hold values 0 or 1
Outputs:
- chi: float32 [128, 128], P(('row', 'col'))
All inputs are finite; a program needn't handle non-finite values.
Results may differ from a plain program's by a relative error of at most 0.0041.
Values may be sent and summed in bfloat16 or wider, within the bound.
No kernel may reach another device: no remote copies, remote signals or barrier semaphores. Data moves between devices by JAX's collectives and lax.ppermute only.
A program may use at most 128 MiB of HBM per device.

v0:
```python
import functools

import jax
import jax.numpy as jnp
from jax import lax
from jax.experimental import pallas as pl
from jax.experimental.pallas import tpu as pltpu
from jax.sharding import PartitionSpec as P


CHUNKS = 4


def chunk_sizes(count):
    last = max(1, count // 8)
    parts = CHUNKS - 1
    return [(count - last + parts - 1 - i) // parts for i in range(parts)] + [last]


def xor_bits(size):
    bits = []
    bit = size // 2
    while bit:
        bits.append(bit)
        bit //= 2
    return bits


def gather_bits(size):
    bits = xor_bits(size)
    return bits[-1:] + bits[:-1]


def swap(value, axis, size, bit):
    return lax.ppermute(value, axis, [(i, i ^ bit) for i in range(size)])


def join(held, other, upper, axis):
    return jnp.stack(
        [jnp.where(upper, other, held), jnp.where(upper, held, other)], axis=axis
    )


def plan_kernel(row_size, p_tiles, caps, me, mask_ref, tile_ref, on_ref, branch_ref):
    tiles, across = mask_ref.shape[1:]
    m_tiles = tiles // row_size
    slots = m_tiles * across

    def used(row, slot):
        found = 0
        for p in range(p_tiles):
            found |= mask_ref[p, row * m_tiles + slot // across, slot % across]
        return (found != 0).astype(jnp.int32)

    most = 0
    for row in range(row_size):
        most = jnp.maximum(most, sum(used(row, slot) for slot in range(slots)))
    branch_ref[0] = sum((most > cap).astype(jnp.int32) for cap in caps[:-1])
    front = 0
    back = sum(used(me[1], slot) for slot in range(slots))
    for slot in range(slots):
        here = used(me[1], slot)
        at = jnp.where(here != 0, front, back)
        tile_ref[at] = slot
        on_ref[at] = mask_ref[me[2], me[1] * m_tiles + slot // across, slot % across]
        front += here
        back += 1 - here


def plan(b_mask, me, row_size, caps):
    p_tiles, tiles, across = b_mask.shape
    slots = tiles // row_size * across
    small = pl.BlockSpec(memory_space=pltpu.SMEM)
    return pl.pallas_call(
        functools.partial(plan_kernel, row_size, p_tiles, caps),
        out_shape=[jax.ShapeDtypeStruct((size,), jnp.int32) for size in (slots, slots, 1)],
        in_specs=[small, small],
        out_specs=[small] * 3,
    )(me, b_mask)


def pack_kernel(near, slots, tile, across, me, slot_tile, slot_on, b_ref, *refs):
    out_refs, wide = refs[:-1], refs[-1]
    wide[...] = b_ref[0].astype(jnp.float32)
    cols = len(out_refs) if near else out_refs[0].shape[0]
    rows = tile // cols

    @pl.loop(0, slots)
    def _(slot):
        top = (slot_tile[slot] // across) * tile
        lane = pl.multiple_of((slot_tile[slot] % across) * tile, tile)
        for k in range(cols):
            start = top + ((me[0] ^ k) if near else k) * rows
            block = wide[pl.ds(pl.multiple_of(start, rows), rows), pl.ds(lane, tile)]
            block = jnp.where(slot_on[slot] != 0, block, 0.0).astype(b_ref.dtype)
            if near:
                out_refs[k][slot, 0] = block
            else:
                out_refs[0][k, slot, 0] = block


def pack(b, first, count, near, me, slot_tile, slot_on, cols, tile):
    _, m_count, n_basis = b.shape
    slots = slot_tile.shape[0]
    rows = tile // cols
    if near:
        out_shape = [jax.ShapeDtypeStruct((slots, count, rows, tile), b.dtype)] * cols
        out_specs = [pl.BlockSpec((slots, 1, rows, tile), lambda p, *_: (0, p, 0, 0))] * cols
    else:
        out_shape = [jax.ShapeDtypeStruct((cols, slots, count, rows, tile), b.dtype)]
        out_specs = [pl.BlockSpec((cols, slots, 1, rows, tile), lambda p, *_: (0, 0, p, 0, 0))]
    return pl.pallas_call(
        functools.partial(pack_kernel, near, slots, tile, n_basis // tile),
        out_shape=out_shape,
        grid_spec=pltpu.PrefetchScalarGridSpec(
            num_scalar_prefetch=3,
            grid=(count,),
            in_specs=[pl.BlockSpec((1, m_count, n_basis), lambda p, *_: (p + first, 0, 0))],
            out_specs=out_specs,
            scratch_shapes=[pltpu.VMEM((m_count, n_basis), jnp.float32)],
        ),
    )(me, slot_tile, slot_on, b)


def lane_block(n_basis):
    return min(256, n_basis)


def keep_tiles(mask_ref, first, tile, value_ref, out_ref):
    rows, lanes = out_ref.shape

    @pl.loop(0, rows // tile)
    def _(i):
        down = pl.ds(pl.multiple_of(i * tile, tile), tile)
        for j in range(lanes // tile):
            at = (down, slice(j * tile, (j + 1) * tile))
            kept = value_ref[at]
            out_ref[at] = jnp.where(mask_ref[first + i, j] != 0, kept, jnp.zeros_like(kept))


def mask_kernel(tile, first, mask_ref, value_ref, out_ref):
    keep_tiles(mask_ref, first[0], tile, value_ref, out_ref)


def masked_tiles(value, mask, first, tile):
    return pl.pallas_call(
        functools.partial(mask_kernel, tile),
        out_shape=jax.ShapeDtypeStruct(value.shape, value.dtype),
        grid_spec=pltpu.PrefetchScalarGridSpec(
            num_scalar_prefetch=2,
            grid=(),
            in_specs=[pl.BlockSpec(memory_space=pltpu.VMEM)],
            out_specs=pl.BlockSpec(memory_space=pltpu.VMEM),
        ),
    )(jnp.reshape(first, (1,)), mask, value)


def inner_kernel(tile, starts, sizes, mask_ref, b_ref, virt_ref, *refs):
    out_refs, masked = refs[:-1], refs[-1]
    keep_tiles(mask_ref, 0, tile, b_ref.at[0], masked)
    n_basis = masked.shape[1]
    width = lane_block(n_basis)
    p = pl.program_id(0)

    @pl.loop(0, n_basis // width)
    def _(j):
        lanes = pl.ds(pl.multiple_of(j * width, width), width)
        part = jnp.dot(
            masked[...], virt_ref[:, lanes], preferred_element_type=jnp.float32
        ).astype(masked.dtype)
        for start, size, out_ref in zip(starts, sizes, out_refs):

            @pl.when((p >= start) & (p < start + size))
            def _():
                out_ref[0, :, lanes] = part


def inner(b, first, sizes, mask, virt, tile):
    _, rows, n_basis = b.shape
    starts = [sum(sizes[:i]) for i in range(len(sizes))]
    return pl.pallas_call(
        functools.partial(inner_kernel, tile, starts, sizes),
        out_shape=[jax.ShapeDtypeStruct((size, rows, n_basis), b.dtype) for size in sizes],
        grid_spec=pltpu.PrefetchScalarGridSpec(
            num_scalar_prefetch=1,
            grid=(sum(sizes),),
            in_specs=[
                pl.BlockSpec((1, rows, n_basis), lambda p, mask: (p + first, 0, 0)),
                pl.BlockSpec((n_basis, n_basis), lambda p, mask: (0, 0)),
            ],
            out_specs=[
                pl.BlockSpec(
                    (1, rows, n_basis),
                    lambda p, mask, start=start, size=size: (
                        jnp.clip(p - start, 0, size - 1),
                        0,
                        0,
                    ),
                )
                for start, size in zip(starts, sizes)
            ],
            scratch_shapes=[pltpu.VMEM((rows, n_basis), b.dtype)],
        ),
    )(mask, b, virt)


def outer_kernel(offsets, slots, tile, across, me, slot_tile, occ_ref, *refs):
    half_refs = refs[: len(offsets)]
    out_refs, wide = refs[len(offsets) : -1], refs[-1]
    depth = half_refs[0].shape[1]
    rows = out_refs[0].shape[2]
    width = lane_block(wide.shape[1])

    @pl.loop(0, wide.shape[1] // width)
    def _(j):
        lanes = pl.ds(pl.multiple_of(j * width, width), width)
        total = None
        for offset, half_ref in zip(offsets, half_refs):
            start = pl.multiple_of((me[1] ^ offset) * depth, depth)
            part = jnp.dot(
                occ_ref[:, pl.ds(start, depth)],
                half_ref[0, :, lanes],
                preferred_element_type=jnp.float32,
            )
            total = part if total is None else total + part
        wide[:, lanes] = total

    @pl.loop(0, slots)
    def _(slot):
        top = (slot_tile[slot] // across) * tile
        lane = pl.multiple_of((slot_tile[slot] % across) * tile, tile)
        for k, out_ref in enumerate(out_refs):
            start = pl.multiple_of(top + (me[0] ^ k) * rows, rows)
            block = wide[pl.ds(start, rows), pl.ds(lane, tile)]
            out_ref[slot, 0] = block.astype(out_ref.dtype)


def outer(occ, halves, offsets, me, slot_tile, cols, tile):
    count, depth, n_basis = halves[0].shape
    slots = slot_tile.shape[0]
    strip = (slots, count, tile // cols, tile)
    return pl.pallas_call(
        functools.partial(outer_kernel, offsets, slots, tile, n_basis // tile),
        out_shape=[jax.ShapeDtypeStruct(strip, occ.dtype)] * cols,
        grid_spec=pltpu.PrefetchScalarGridSpec(
            num_scalar_prefetch=2,
            grid=(count,),
            in_specs=[pl.BlockSpec(occ.shape, lambda p, me, which: (0, 0))]
            + [pl.BlockSpec((1, depth, n_basis), lambda p, me, which: (p, 0, 0))] * len(halves),
            out_specs=[
                pl.BlockSpec((slots, 1) + strip[2:], lambda p, me, which: (0, p, 0, 0))
            ]
            * cols,
            scratch_shapes=[pltpu.VMEM((occ.shape[0], n_basis), jnp.float32)],
        ),
    )(me, slot_tile, occ, *halves)


def group_of(slots):
    groups = [size for size in range(2, 9) if slots % size == 0]
    return max(groups, default=slots)


def place(me, strips, slot, wide, base, stride):
    for k, ref in enumerate(strips):
        count = ref.shape[1]
        wide[pl.ds((me[0] ^ k) * stride + base, count)] = ref[slot].astype(jnp.float32)


def unroll_rows(wide, out_ref, start):
    turned = jnp.swapaxes(wide[...], 0, 1).astype(out_ref.dtype)
    rows, _, lanes = turned.shape
    for row in range(rows):
        at = start + row * lanes
        at = at if isinstance(at, int) else pl.multiple_of(at, lanes)
        out_ref[:, pl.ds(at, lanes)] = turned[row]


def flatten_kernel(group, early, me, *refs):
    near_refs, rest_ref, out_ref, wide = refs[:-3], refs[-3], refs[-2], refs[-1]
    cols, _, late, rows, lanes = rest_ref.shape

    @pl.loop(0, group)
    def _(slot):
        place(me, near_refs, slot, wide, 0, early + late)
        for k in range(cols):
            start = k * (early + late) + early
            wide[start : start + late] = rest_ref[k, slot].astype(jnp.float32)
        unroll_rows(wide, out_ref, slot * (rows * lanes))


def flatten(near, rest, me):
    cols, slots, late, rows, lanes = rest.shape
    early = near[0].shape[1]
    total = cols * (early + late)
    group = group_of(slots)
    return pl.pallas_call(
        functools.partial(flatten_kernel, group, early),
        out_shape=jax.ShapeDtypeStruct((total, slots * rows * lanes), rest.dtype),
        grid_spec=pltpu.PrefetchScalarGridSpec(
            num_scalar_prefetch=1,
            grid=(slots // group,),
            in_specs=[pl.BlockSpec((group, early, rows, lanes), lambda s, me: (s, 0, 0, 0))]
            * cols
            + [pl.BlockSpec((cols, group, late, rows, lanes), lambda s, me: (0, s, 0, 0, 0))],
            out_specs=pl.BlockSpec((total, group * rows * lanes), lambda s, me: (0, s)),
            scratch_shapes=[pltpu.VMEM((total, rows, lanes), jnp.float32)],
        ),
    )(me, *near, rest)


def contract_kernel(group, counts, cols, me, *refs):
    strips, b_ref, out_ref, wide, flat = refs[:-4], *refs[-4:]
    width = flat.shape[1]

    @pl.when(pl.program_id(0) == 0)
    def _():
        out_ref[...] = jnp.zeros_like(out_ref)

    @pl.loop(0, group)
    def _(slot):
        base = 0
        for i, count in enumerate(counts):
            place(me, strips[i * cols : (i + 1) * cols], slot, wide, base, sum(counts))
            base += count
        unroll_rows(wide, flat, 0)
        out_ref[...] += lax.dot_general(
            flat[...],
            b_ref[:, pl.ds(pl.multiple_of(slot * width, width), width)],
            (((1,), (1,)), ((), ())),
            preferred_element_type=jnp.float32,
        )


def contract(chunks, b_flat, me):
    cols = len(chunks[0])
    slots, _, rows, lanes = chunks[0][0].shape
    counts = [chunk[0].shape[1] for chunk in chunks]
    total, width = cols * sum(counts), rows * lanes
    group = group_of(slots)
    return pl.pallas_call(
        functools.partial(contract_kernel, group, counts, cols),
        out_shape=jax.ShapeDtypeStruct((total, b_flat.shape[0]), jnp.float32),
        grid_spec=pltpu.PrefetchScalarGridSpec(
            num_scalar_prefetch=1,
            grid=(slots // group,),
            in_specs=[
                pl.BlockSpec((group, count, rows, lanes), lambda s, me: (s, 0, 0, 0))
                for count in counts
                for _ in range(cols)
            ]
            + [pl.BlockSpec((b_flat.shape[0], group * width), lambda s, me: (0, s))],
            out_specs=pl.BlockSpec((total, b_flat.shape[0]), lambda s, me: (0, 0)),
            scratch_shapes=[
                pltpu.VMEM((total, rows, lanes), jnp.float32),
                pltpu.VMEM((total, width), b_flat.dtype),
            ],
        ),
    )(me, *[strip for chunk in chunks for strip in chunk], b_flat)


def exchange(strips):
    return [strips[0]] + [swap(s, "col", len(strips), k) for k, s in enumerate(strips) if k]


def per_device(row_size, col_size, b_tensor, occ_green, virt_green, b_mask, occ_mask, virt_mask):
    p_count, m_count, n_basis = b_tensor.shape
    tile = n_basis // b_mask.shape[2]
    col_index, row_index = lax.axis_index("col"), lax.axis_index("row")
    me = jnp.stack([col_index, row_index, (col_index * p_count) // tile]).astype(jnp.int32)
    caps = slot_caps(m_count // tile * (n_basis // tile))
    slot_tile, slot_on, branch = plan(b_mask, me, row_size, caps)

    def with_slots(cap, *args):
        return run(row_size, col_size, tile, slot_tile[:cap], slot_on[:cap], me, *args)

    return lax.switch(
        branch[0],
        [functools.partial(with_slots, cap) for cap in caps],
        b_tensor,
        occ_green,
        virt_green,
        b_mask,
        occ_mask,
        virt_mask,
    )


def slot_caps(slots):
    return sorted({slots * part // 16 for part in (13, 14, 16)})


def run(
    row_size,
    col_size,
    tile,
    slot_tile,
    slot_on,
    me,
    b_tensor,
    occ_green,
    virt_green,
    b_mask,
    occ_mask,
    virt_mask,
):
    col_index, row_index = me[0], me[1]
    p_count, m_count, n_basis = b_tensor.shape
    m_tiles = m_count // tile
    across = n_basis // tile
    local_mask = lax.dynamic_slice(b_mask, (me[2], row_index * m_tiles, 0), (1, m_tiles, across))[0]

    green, seen = jnp.stack([virt_green, occ_green]), []
    for bit in gather_bits(col_size):
        upper = (col_index & bit) != 0
        axis = 1 + sum(other > bit for other in seen)
        seen.append(bit)
        green = join(green, swap(green, "col", col_size, bit), upper, axis)
    virt_rows, occ_rows = green.reshape(2, -1, n_basis)

    early = max(1, p_count // 8)
    strips = pack(b_tensor, 0, early, True, me, slot_tile, slot_on, col_size, tile)
    near = exchange(strips)
    (strips,) = pack(
        b_tensor, early, p_count - early, False, me, slot_tile, slot_on, col_size, tile
    )
    rest = lax.all_to_all(strips, "col", split_axis=0, concat_axis=0, tiled=True)

    virt = virt_rows
    for depth, bit in enumerate(xor_bits(row_size)):
        upper = (row_index & bit) != 0
        virt = join(virt, swap(virt, "row", row_size, bit), upper, depth)
    virt = masked_tiles(virt.reshape(n_basis, n_basis), virt_mask, 0, tile)
    occ = masked_tiles(occ_rows, occ_mask, row_index * m_tiles, tile)

    sizes = chunk_sizes(p_count)
    offsets = [0]
    for bit in xor_bits(row_size):
        offsets = offsets + [offset ^ bit for offset in offsets]
    ready = inner(b_tensor, 0, sizes[:1], local_mask, virt, tile)
    ready += inner(b_tensor, sizes[0], sizes[1:], local_mask, virt, tile)
    gathered = []
    for k in range(CHUNKS):
        halves = [ready[k]]
        for bit in xor_bits(row_size):
            halves = halves + [swap(h, "row", row_size, bit) for h in halves]
        gathered.append(halves)
    moved = []
    for k in range(CHUNKS):
        strips = outer(occ, gathered[k], offsets, me, slot_tile, col_size, tile)
        moved.append(exchange(strips))

    b_flat = flatten(near, rest, me)
    sums = []
    sums.append(contract(moved[:-1], b_flat, me))
    sums.append(contract(moved[-1:], b_flat, me))
    sums = [part.reshape(col_size, -1, part.shape[-1]) for part in sums]
    total = jnp.concatenate(sums, axis=1)
    total = total.reshape(row_size * col_size, -1, total.shape[-1])
    shares = lax.all_to_all(total, ("row", "col"), split_axis=0, concat_axis=0, tiled=True)
    return shares.sum(0) * (-2.0 / n_basis)


def solution(mesh):
    row_size, col_size = mesh.shape["row"], mesh.shape["col"]

    return jax.shard_map(
        functools.partial(per_device, row_size, col_size),
        mesh=mesh,
        in_specs=(
            P("col", "row", None),
            P(("row", "col"), None),
            P(("row", "col"), None),
            P(),
            P(),
            P(),
        ),
        out_specs=P(("row", "col"), None),
        check_vma=False,
    )
```

profile of v0, /device:TPU:1, one launch (start us, length us, event | category | flops | bytes accessed | tf_op | source)
XLA Modules:
  0.0 597.9 jit_solution(12141232494533698345)
XLA Ops:
  2.2 595.1 %conditional.1 = (f32[4,128]{1,0:T(4,128)S(1)}) conditional(s32[]{:T(128)} %bitcast.78, (s32[16]{0:T(128)S(1)}, s32[]{:T(128)}, s32[]{:T(128)}, bf16[32,1024]{1,0:T(8,128)(2,1)}, bf16[32,1024]{1,0:T(8,128)(2,1)}, /*index=5*/s32[8,8]{1,0:T(8,128)}, s32[1,8,8]{2,1,0:T(8,128)}, s32[8,8]{1,0:T(8,128)}, bf16[16,256,1024]{2,1,0:T(8,128)(2,1)}, ...), branch_computations={%region_0.2_spmd, %region_2.4_spmd, %region_4.6_spmd} | conditional | flops 6062094 | bytes 238480608 | solution.py:377
  11.7 14.1 %branch_0_fun.21 = bf16[8,13,14,16,128]{4,3,2,1,0:T(8,128)(2,1)} custom-call(s32[3]{0:T(128)S(1)} %get-tuple-element.78.me, s32[13]{0:T(128)S(1)} %bitcast.146, s32[13]{0:T(128)S(1)} %bitcast.161, bf16[16,256,1024]{2,1,0:T(8,128)(2,1)} %get-tuple-element.86.b_ref), custom_call_target="tpu_custom_call" | custom-call | tf_op jit(solution)/shard_map/cond/branch_0_fun/pallas_call | solution.py:112
  25.8 4.7 all-to-all-start
  32.0 105.0 %collective-permute-done.2 = bf16[2,2,2,32,1024]{4,3,2,1,0:T(8,128)(2,1)S(1)} collective-permute-done((bf16[2,2,2,32,1024]{4,3,2,1,0:T(8,128)(2,1)S(1)}, bf16[2,2,2,32,1024]{4,3,2,1,0:T(8,128)(2,1)S(1)}, u32[]{:S(2)}, u32[]{:S(2)}) %collective-permute-start.2) | collective-permute-done | bytes 524320 | tf_op jit(solution)/shard_map/cond/branch_0_fun/ppermute | solution.py:35
  139.2 10.0 %collective-permute-done.3 = bf16[256,1024]{1,0:T(8,128)(2,1)S(1)} collective-permute-done((bf16[256,1024]{1,0:T(8,128)(2,1)S(1)}, bf16[256,1024]{1,0:T(8,128)(2,1)S(1)}, u32[]{:S(2)}, u32[]{:S(2)}) %collective-permute-start.3) | collective-permute-done | bytes 524320 | tf_op jit(solution)/shard_map/cond/branch_0_fun/ppermute | solution.py:35
  156.7 4.2 branch_0_fun.14.virt_ref
  160.9 20.9 %branch_0_fun.17 = (bf16[5,256,1024]{2,1,0:T(8,128)(2,1)}, bf16[4,256,1024]{2,1,0:T(8,128)(2,1)}, bf16[2,256,1024]{2,1,0:T(8,128)(2,1)}) custom-call(s32[2,8]{1,0:T(2,128)} %dynamic-slice_bitcast_fusion.mask_ref, bf16[16,256,1024]{2,1,0:T(8,128)(2,1)} %get-tuple-element.86.b_ref, bf16[1024,1024]{1,0:T(8,128)(2,1)} %branch_0_fun.14.virt_ref), custom_call_target="tpu_custom_call" | custom-call | tf_op jit(solution)/shard_map/cond/branch_0_fun/pallas_call | solution.py:181
  182.1 10.7 %branch_0_fun.15.refs_0_ = bf16[5,256,1024]{2,1,0:T(8,128)(2,1)} custom-call(s32[2,8]{1,0:T(2,128)} %dynamic-slice_bitcast_fusion.mask_ref, bf16[16,256,1024]{2,1,0:T(8,128)(2,1)} %get-tuple-element.86.b_ref, bf16[1024,1024]{1,0:T(8,128)(2,1)} %branch_0_fun.14.virt_ref), custom_call_target="tpu_custom_call" | custom-call | tf_op jit(solution)/shard_map/cond/branch_0_fun/pallas_call | solution.py:181
  194.1 3.7 branch_0_fun.20
  210.1 7.5 %collective-permute-done.39.refs_5_ = bf16[13,2,16,128]{3,2,1,0:T(8,128)(2,1)S(1)} collective-permute-done((bf16[13,2,16,128]{3,2,1,0:T(8,128)(2,1)}, bf16[13,2,16,128]{3,2,1,0:T(8,128)(2,1)S(1)}, u32[]{:S(2)}, u32[]{:S(2)}) %collective-permute-start.39) | collective-permute-done | bytes 106528 | tf_op jit(solution)/shard_map/cond/branch_0_fun/ppermute | solution.py:35
  221.2 4.8 collective-permute-done.41.refs_7_
  227.4 102.6 %collective-permute-done.42.refs_1_ = bf16[2,256,1024]{2,1,0:T(8,128)(2,1)S(1)} collective-permute-done((bf16[2,256,1024]{2,1,0:T(8,128)(2,1)}, bf16[2,256,1024]{2,1,0:T(8,128)(2,1)S(1)}, u32[]{:S(2)}, u32[]{:S(2)}) %collective-permute-start.42) | collective-permute-done | bytes 1048608 | tf_op jit(solution)/shard_map/cond/branch_0_fun/ppermute | solution.py:35
  337.8 6.9 %branch_0_fun.24 = (bf16[13,2,16,128]{3,2,1,0:T(8,128)(2,1)}, bf16[13,2,16,128]{3,2,1,0:T(8,128)(2,1)}, bf16[13,2,16,128]{3,2,1,0:T(8,128)(2,1)}, bf16[13,2,16,1...) custom-call(s32[3]{0:T(128)S(1)} %get-tuple-element.78.me, ...), custom_call_target="tpu_custom_call" | custom-call | tf_op jit(solution)/shard_map/cond/branch_0_fun/pallas_call | solution.py:242
  344.7 30.3 %collective-permute-done.25.refs_1_ = bf16[4,256,1024]{2,1,0:T(8,128)(2,1)} collective-permute-done((bf16[4,256,1024]{2,1,0:T(8,128)(2,1)}, bf16[4,256,1024]{2,1,0:T(8,128)(2,1)}, u32[]{:S(2)}, u32[]{:S(2)}) %collective-permute-start.25) | collective-permute-done | bytes 2097184 | tf_op jit(solution)/shard_map/cond/branch_0_fun/ppermute | solution.py:35
  381.0 4.1 collective-permute-done.27.refs_3_
  387.4 10.8 %branch_0_fun.19 = (bf16[13,4,16,128]{3,2,1,0:T(8,128)(2,1)}, bf16[13,4,16,128]{3,2,1,0:T(8,128)(2,1)}, bf16[13,4,16,128]{3,2,1,0:T(8,128)(2,1)}, bf16[13,4,16,1...) custom-call(s32[3]{0:T(128)S(1)} %get-tuple-element.78.me, ...), custom_call_target="tpu_custom_call" | custom-call | tf_op jit(solution)/shard_map/cond/branch_0_fun/pallas_call | solution.py:242
  400.9 3.8 collective-permute-done.28.refs_17_
  410.3 12.6 %branch_0_fun.16 = (bf16[13,5,16,128]{3,2,1,0:T(8,128)(2,1)}, bf16[13,5,16,128]{3,2,1,0:T(8,128)(2,1)}, bf16[13,5,16,128]{3,2,1,0:T(8,128)(2,1)}, bf16[13,5,16,1...) custom-call(s32[3]{0:T(128)S(1)} %get-tuple-element.78.me, ...), custom_call_target="tpu_custom_call" | custom-call | tf_op jit(solution)/shard_map/cond/branch_0_fun/pallas_call | solution.py:242
  425.8 4.3 collective-permute-done.32.refs_21_
  432.0 4.7 collective-permute-start.11
  438.0 12.7 %branch_0_fun.18 = (bf16[13,5,16,128]{3,2,1,0:T(8,128)(2,1)}, bf16[13,5,16,128]{3,2,1,0:T(8,128)(2,1)}, bf16[13,5,16,128]{3,2,1,0:T(8,128)(2,1)}, bf16[13,5,16,1...) custom-call(s32[3]{0:T(128)S(1)} %get-tuple-element.78.me, ...), custom_call_target="tpu_custom_call" | custom-call | tf_op jit(solution)/shard_map/cond/branch_0_fun/pallas_call | solution.py:242
  450.7 6.7 %collective-permute-start.12 = (bf16[13,5,16,128]{3,2,1,0:T(8,128)(2,1)S(1)}, bf16[13,5,16,128]{3,2,1,0:T(8,128)(2,1)S(1)}, u32[]{:S(2)}, u32[]{:S(2)}) collective-permute-start(bf16[13,5,16,128]{3,2,1,0:T(8,128)(2,1)S(1)} %copy-done.107), channel_id=1, source_target_pairs={{0,5},{1,4},{2,7},{3,6},{4,1},{5,0},{6,3},{7,2},{8,13},{9,12},{10,... | collective-permute-start | bytes 798728 | tf_op jit(solution)/shard_map/cond/branch_0_fun/ppermute | solution.py:35
  462.1 15.6 %collective-permute-done.12.refs_5_ = bf16[13,5,16,128]{3,2,1,0:T(8,128)(2,1)S(1)} collective-permute-done((bf16[13,5,16,128]{3,2,1,0:T(8,128)(2,1)S(1)}, bf16[13,5,16,128]{3,2,1,0:T(8,128)(2,1)S(1)}, u32[]{:S(2)}, u32[]{:S(2)}) %collective-permute-start.12) | collective-permute-done | bytes 266272 | tf_op jit(solution)/shard_map/cond/branch_0_fun/ppermute | solution.py:35
  480.6 8.6 %collective-permute-start.21 = (bf16[13,5,16,128]{3,2,1,0:T(8,128)(2,1)}, bf16[13,5,16,128]{3,2,1,0:T(8,128)(2,1)S(1)}, u32[]{:S(2)}, u32[]{:S(2)}) collective-permute-start(bf16[13,5,16,128]{3,2,1,0:T(8,128)(2,1)} %get-tuple-element.101), channel_id=1, source_target_pairs={{0,4},{1,5},{2,6},{3,7},{4,0},{5,1},{6,2},{7,3},{8,12},{9,13},{10,... | collective-permute-start | bytes 798728 | tf_op jit(solution)/shard_map/cond/branch_0_fun/ppermute | solution.py:35
  489.3 13.6 %collective-permute-start.22 = (bf16[13,5,16,128]{3,2,1,0:T(8,128)(2,1)}, bf16[13,5,16,128]{3,2,1,0:T(8,128)(2,1)S(1)}, u32[]{:S(2)}, u32[]{:S(2)}) collective-permute-start(bf16[13,5,16,128]{3,2,1,0:T(8,128)(2,1)} %get-tuple-element.102), channel_id=1, source_target_pairs={{0,5},{1,4},{2,7},{3,6},{4,1},{5,0},{6,3},{7,2},{8,13},{9,12},{10,... | collective-permute-start | bytes 798728 | tf_op jit(solution)/shard_map/cond/branch_0_fun/ppermute | solution.py:35
  507.4 21.2 %collective-permute-done.22.refs_13_ = bf16[13,5,16,128]{3,2,1,0:T(8,128)(2,1)S(1)} collective-permute-done((bf16[13,5,16,128]{3,2,1,0:T(8,128)(2,1)}, bf16[13,5,16,128]{3,2,1,0:T(8,128)(2,1)S(1)}, u32[]{:S(2)}, u32[]{:S(2)}) %collective-permute-start.22) | collective-permute-done | bytes 266272 | tf_op jit(solution)/shard_map/cond/branch_0_fun/ppermute | solution.py:35
  528.6 3.7 collective-permute-start.50
  532.3 3.6 collective-permute-start.51
  535.9 11.0 %branch_0_fun.22.refs_24_.refs_8_ = bf16[128,26624]{1,0:T(8,128)(2,1)} custom-call(s32[3]{0:T(128)S(1)} %get-tuple-element.78.me, bf16[13,2,16,128]{3,2,1,0:T(8,128)(2,1)} %get-tuple-element.115.refs_0_, bf16[13,2,16,128]{3,2,1,0:T(8,128)(2,1)} %copy-done.88, bf16[13,2,16,128]{3,2,1,0:T(8,128)(2,1)} %copy-done.89, bf16[13,2,16,128]{3,2,1,0:T(8,128)(2,1)} %copy-done.90, ...), custom_call_target="tpu_custom_call" | custom-call | tf_op jit(solution)/shard_map/cond/branch_0_fun/pallas_call | solution.py:297
  547.0 12.3 %branch_0_fun.23 = f32[112,128]{1,0:T(8,128)} custom-call(s32[3]{0:T(128)S(1)} %get-tuple-element.78.me, bf16[13,5,16,128]{3,2,1,0:T(8,128)(2,1)} %get-tuple-element.88.refs_0_, bf16[13,5,16,128]{3,2,1,0:T(8,128)(2,1)} %copy-done.36, bf16[13,5,16,128]{3,2,1,0:T(8,128)(2,1)} %copy-done.37, bf16[13,5,16,128]{3,2,1,0:T(8,128)(2,1)} %copy-done.38, ...), custom_call_target="tpu_custom_call" | custom-call | tf_op jit(solution)/shard_map/cond/branch_0_fun/pallas_call | solution.py:341
  560.8 7.8 %branch_0_fun.25 = f32[16,128]{1,0:T(8,128)} custom-call(s32[3]{0:T(128)S(1)} %get-tuple-element.78.me, bf16[13,2,16,128]{3,2,1,0:T(8,128)(2,1)} %get-tuple-element.124.refs_0_, bf16[13,2,16,128]{3,2,1,0:T(8,128)(2,1)} %copy-done.85, bf16[13,2,16,128]{3,2,1,0:T(8,128)(2,1)} %copy-done.86, bf16[13,2,16,128]{3,2,1,0:T(8,128)(2,1)} %copy-done.87, ...), custom_call_target="tpu_custom_call" | custom-call | tf_op jit(solution)/shard_map/cond/branch_0_fun/pallas_call | solution.py:341
  569.3 27.7 %all_to_all.24 = f32[32,4,128]{2,1,0:T(4,128)S(1)} all-to-all(f32[32,4,128]{2,1,0:T(4,128)S(1)} %bitcast.143), channel_id=1, replica_groups=mesh['row'=4,'col'=8] {'row','col'}, dimensions={0} | all-to-all | bytes 131072 | tf_op jit(solution)/shard_map/cond/branch_0_fun/all_to_all | solution.py:460
  (186 shorter events, 86.5 us)
Async XLA Ops:
  25.8 510.1 %all-to-all-start = ((bf16[8,13,14,16,128]{4,3,2,1,0:T(8,128)(2,1)}), bf16[8,13,14,16,128]{4,3,2,1,0:T(8,128)(2,1)}, u32[]{:S(2)}, u32[]{:S(2)}) async-start(bf16[8,13,14,16,128]{4,3,2,1,0:T(8,128)(2,1)} %branch_0_fun.21), calls=%async_computation | async-start | bytes 11927552 | tf_op jit(solution)/shard_map/cond/branch_0_fun/all_to_all | solution.py:427
  30.6 106.3 %collective-permute-start.2 = (bf16[2,2,2,32,1024]{4,3,2,1,0:T(8,128)(2,1)S(1)}, bf16[2,2,2,32,1024]{4,3,2,1,0:T(8,128)(2,1)S(1)}, u32[]{:S(2)}, u32[]{:S(2)}) collective-permute-start(bf16[2,2,2,32,1024]{4,3,2,1,0:T(8,128)(2,1)S(1)} %pad_maximum_fusion.3), channel_id=1, source_target_pairs={{0,2},{1,3},{2,0},{3,1},{4,6},{5,7},{6,4},{7,5},{8,10},{9,11},{10,... | collective-permute-start | bytes 1572872 | tf_op jit(solution)/shard_map/cond/branch_0_fun/ppermute | solution.py:35
  181.8 44.4 %collective-permute-start.43 = (bf16[2,256,1024]{2,1,0:T(8,128)(2,1)}, bf16[2,256,1024]{2,1,0:T(8,128)(2,1)}, u32[]{:S(2)}, u32[]{:S(2)}) collective-permute-start(bf16[2,256,1024]{2,1,0:T(8,128)(2,1)} %get-tuple-element.123.refs_0_), channel_id=1, source_target_pairs={{0,8},{8,0},{16,24},{24,16},{1,9},{9,1},{17,25},{25,17},{2,10},{10... | collective-permute-start | bytes 3145736 | tf_op jit(solution)/shard_map/cond/branch_0_fun/ppermute | solution.py:35
  192.8 142.0 %collective-permute-start.5 = (bf16[5,256,1024]{2,1,0:T(8,128)(2,1)}, bf16[5,256,1024]{2,1,0:T(8,128)(2,1)}, u32[]{:S(2)}, u32[]{:S(2)}) collective-permute-start(bf16[5,256,1024]{2,1,0:T(8,128)(2,1)} %branch_0_fun.15.refs_0_), channel_id=1, source_target_pairs={{0,16},{8,24},{16,0},{24,8},{1,17},{9,25},{17,1},{25,9},{2,18},{10... | collective-permute-start | bytes 7864328 | tf_op jit(solution)/shard_map/cond/branch_0_fun/ppermute | solution.py:35
  206.7 174.2 %collective-permute-start.15 = (bf16[5,256,1024]{2,1,0:T(8,128)(2,1)}, bf16[5,256,1024]{2,1,0:T(8,128)(2,1)}, u32[]{:S(2)}, u32[]{:S(2)}) collective-permute-start(bf16[5,256,1024]{2,1,0:T(8,128)(2,1)} %get-tuple-element.96.refs_0_), channel_id=1, source_target_pairs={{0,16},{8,24},{16,0},{24,8},{1,17},{9,25},{17,1},{25,9},{2,18},{10... | collective-permute-start | bytes 7864328 | tf_op jit(solution)/shard_map/cond/branch_0_fun/ppermute | solution.py:35
  217.6 114.0 %collective-permute-start.26 = (bf16[4,256,1024]{2,1,0:T(8,128)(2,1)}, bf16[4,256,1024]{2,1,0:T(8,128)(2,1)S(1)}, u32[]{:S(2)}, u32[]{:S(2)}) collective-permute-start(bf16[4,256,1024]{2,1,0:T(8,128)(2,1)} %get-tuple-element.105.refs_0_), channel_id=1, source_target_pairs={{0,8},{8,0},{16,24},{24,16},{1,9},{9,1},{17,25},{25,17},{2,10},{10... | collective-permute-start | bytes 6291464 | tf_op jit(solution)/shard_map/cond/branch_0_fun/ppermute | solution.py:35
  225.9 104.0 %collective-permute-start.42 = (bf16[2,256,1024]{2,1,0:T(8,128)(2,1)}, bf16[2,256,1024]{2,1,0:T(8,128)(2,1)S(1)}, u32[]{:S(2)}, u32[]{:S(2)}) collective-permute-start(bf16[2,256,1024]{2,1,0:T(8,128)(2,1)} %get-tuple-element.123.refs_0_), channel_id=1, source_target_pairs={{0,16},{8,24},{16,0},{24,8},{1,17},{9,25},{17,1},{25,9},{2,18},{10... | collective-permute-start | bytes 3145736 | tf_op jit(solution)/shard_map/cond/branch_0_fun/ppermute | solution.py:35
  226.2 148.8 %collective-permute-start.25 = (bf16[4,256,1024]{2,1,0:T(8,128)(2,1)}, bf16[4,256,1024]{2,1,0:T(8,128)(2,1)}, u32[]{:S(2)}, u32[]{:S(2)}) collective-permute-start(bf16[4,256,1024]{2,1,0:T(8,128)(2,1)} %get-tuple-element.105.refs_0_), channel_id=1, source_target_pairs={{0,16},{8,24},{16,0},{24,8},{1,17},{9,25},{17,1},{25,9},{2,18},{10... | collective-permute-start | bytes 6291464 | tf_op jit(solution)/shard_map/cond/branch_0_fun/ppermute | solution.py:35
  331.6 67.7 %collective-permute-start.6 = (bf16[5,256,1024]{2,1,0:T(8,128)(2,1)S(1)}, bf16[5,256,1024]{2,1,0:T(8,128)(2,1)}, u32[]{:S(2)}, u32[]{:S(2)}) collective-permute-start(bf16[5,256,1024]{2,1,0:T(8,128)(2,1)S(1)} %copy-done), channel_id=1, source_target_pairs={{0,8},{8,0},{16,24},{24,16},{1,9},{9,1},{17,25},{25,17},{2,10},{10... | collective-permute-start | bytes 7864328 | tf_op jit(solution)/shard_map/cond/branch_0_fun/ppermute | solution.py:35
  333.9 65.4 %collective-permute-start.16 = (bf16[5,256,1024]{2,1,0:T(8,128)(2,1)}, bf16[5,256,1024]{2,1,0:T(8,128)(2,1)}, u32[]{:S(2)}, u32[]{:S(2)}) collective-permute-start(bf16[5,256,1024]{2,1,0:T(8,128)(2,1)} %get-tuple-element.96.refs_0_), channel_id=1, source_target_pairs={{0,8},{8,0},{16,24},{24,16},{1,9},{9,1},{17,25},{25,17},{2,10},{10... | collective-permute-start | bytes 7864328 | tf_op jit(solution)/shard_map/cond/branch_0_fun/ppermute | solution.py:35
  334.8 73.0 %collective-permute-start.7 = (bf16[5,256,1024]{2,1,0:T(8,128)(2,1)}, bf16[5,256,1024]{2,1,0:T(8,128)(2,1)}, u32[]{:S(2)}, u32[]{:S(2)}) collective-permute-start(bf16[5,256,1024]{2,1,0:T(8,128)(2,1)} %collective-permute-done.5.refs_1_), channel_id=1, source_target_pairs={{0,8},{8,0},{16,24},{24,16},{1,9},{9,1},{17,25},{25,17},{2,10},{10... | collective-permute-start | bytes 7864328 | tf_op jit(solution)/shard_map/cond/branch_0_fun/ppermute | solution.py:35
  380.9 55.8 %collective-permute-start.17 = (bf16[5,256,1024]{2,1,0:T(8,128)(2,1)}, bf16[5,256,1024]{2,1,0:T(8,128)(2,1)}, u32[]{:S(2)}, u32[]{:S(2)}) collective-permute-start(bf16[5,256,1024]{2,1,0:T(8,128)(2,1)} %collective-permute-done.15.refs_1_), channel_id=1, source_target_pairs={{0,8},{8,0},{16,24},{24,16},{1,9},{9,1},{17,25},{25,17},{2,10},{10... | collective-permute-start | bytes 7864328 | tf_op jit(solution)/shard_map/cond/branch_0_fun/ppermute | solution.py:35
  399.3 23.7 %collective-permute-start.30 = (bf16[13,4,16,128]{3,2,1,0:T(8,128)(2,1)}, bf16[13,4,16,128]{3,2,1,0:T(8,128)(2,1)S(1)}, u32[]{:S(2)}, u32[]{:S(2)}) collective-permute-start(bf16[13,4,16,128]{3,2,1,0:T(8,128)(2,1)} %get-tuple-element.109), channel_id=1, source_target_pairs={{0,3},{1,2},{2,1},{3,0},{4,7},{5,6},{6,5},{7,4},{8,11},{9,10},{10,... | collective-permute-start | bytes 638984 | tf_op jit(solution)/shard_map/cond/branch_0_fun/ppermute | solution.py:35
  406.3 23.8 %collective-permute-start.32 = (bf16[13,4,16,128]{3,2,1,0:T(8,128)(2,1)}, bf16[13,4,16,128]{3,2,1,0:T(8,128)(2,1)S(1)}, u32[]{:S(2)}, u32[]{:S(2)}) collective-permute-start(bf16[13,4,16,128]{3,2,1,0:T(8,128)(2,1)} %get-tuple-element.111), channel_id=1, source_target_pairs={{0,5},{1,4},{2,7},{3,6},{4,1},{5,0},{6,3},{7,2},{8,13},{9,12},{10,... | collective-permute-start | bytes 638984 | tf_op jit(solution)/shard_map/cond/branch_0_fun/ppermute | solution.py:35
  423.7 33.8 %collective-permute-start.8 = (bf16[13,5,16,128]{3,2,1,0:T(8,128)(2,1)}, bf16[13,5,16,128]{3,2,1,0:T(8,128)(2,1)S(1)}, u32[]{:S(2)}, u32[]{:S(2)}) collective-permute-start(bf16[13,5,16,128]{3,2,1,0:T(8,128)(2,1)} %get-tuple-element.89), channel_id=1, source_target_pairs={{0,1},{1,0},{2,3},{3,2},{4,5},{5,4},{6,7},{7,6},{8,9},{9,8},{10,11... | collective-permute-start | bytes 798728 | tf_op jit(solution)/shard_map/cond/branch_0_fun/ppermute | solution.py:35
  424.8 35.5 %collective-permute-start.9 = (bf16[13,5,16,128]{3,2,1,0:T(8,128)(2,1)}, bf16[13,5,16,128]{3,2,1,0:T(8,128)(2,1)S(1)}, u32[]{:S(2)}, u32[]{:S(2)}) collective-permute-start(bf16[13,5,16,128]{3,2,1,0:T(8,128)(2,1)} %get-tuple-element.90), channel_id=1, source_target_pairs={{0,2},{1,3},{2,0},{3,1},{4,6},{5,7},{6,4},{7,5},{8,10},{9,11},{10,... | collective-permute-start | bytes 798728 | tf_op jit(solution)/shard_map/cond/branch_0_fun/ppermute | solution.py:35
  430.8 30.8 %collective-permute-start.10 = (bf16[13,5,16,128]{3,2,1,0:T(8,128)(2,1)}, bf16[13,5,16,128]{3,2,1,0:T(8,128)(2,1)S(1)}, u32[]{:S(2)}, u32[]{:S(2)}) collective-permute-start(bf16[13,5,16,128]{3,2,1,0:T(8,128)(2,1)} %get-tuple-element.91), channel_id=1, source_target_pairs={{0,3},{1,2},{2,1},{3,0},{4,7},{5,6},{6,5},{7,4},{8,11},{9,10},{10,... | collective-permute-start | bytes 798728 | tf_op jit(solution)/shard_map/cond/branch_0_fun/ppermute | solution.py:35
  432.0 30.1 %collective-permute-start.11 = (bf16[13,5,16,128]{3,2,1,0:T(8,128)(2,1)}, bf16[13,5,16,128]{3,2,1,0:T(8,128)(2,1)S(1)}, u32[]{:S(2)}, u32[]{:S(2)}) collective-permute-start(bf16[13,5,16,128]{3,2,1,0:T(8,128)(2,1)} %get-tuple-element.92), channel_id=1, source_target_pairs={{0,4},{1,5},{2,6},{3,7},{4,0},{5,1},{6,2},{7,3},{8,12},{9,13},{10,... | collective-permute-start | bytes 798728 | tf_op jit(solution)/shard_map/cond/branch_0_fun/ppermute | solution.py:35
  450.7 27.0 %collective-permute-start.12 = (bf16[13,5,16,128]{3,2,1,0:T(8,128)(2,1)S(1)}, bf16[13,5,16,128]{3,2,1,0:T(8,128)(2,1)S(1)}, u32[]{:S(2)}, u32[]{:S(2)}) collective-permute-start(bf16[13,5,16,128]{3,2,1,0:T(8,128)(2,1)S(1)} %copy-done.107), channel_id=1, source_target_pairs={{0,5},{1,4},{2,7},{3,6},{4,1},{5,0},{6,3},{7,2},{8,13},{9,12},{10,... | collective-permute-start | bytes 798728 | tf_op jit(solution)/shard_map/cond/branch_0_fun/ppermute | solution.py:35
  460.2 29.0 %collective-permute-start.14 = (bf16[13,5,16,128]{3,2,1,0:T(8,128)(2,1)S(1)}, bf16[13,5,16,128]{3,2,1,0:T(8,128)(2,1)S(1)}, u32[]{:S(2)}, u32[]{:S(2)}) collective-permute-start(bf16[13,5,16,128]{3,2,1,0:T(8,128)(2,1)S(1)} %copy-done.105), channel_id=1, source_target_pairs={{0,7},{1,6},{2,5},{3,4},{4,3},{5,2},{6,1},{7,0},{8,15},{9,14},{10,... | collective-permute-start | bytes 798728 | tf_op jit(solution)/shard_map/cond/branch_0_fun/ppermute | solution.py:35
  461.7 41.2 %collective-permute-start.18 = (bf16[13,5,16,128]{3,2,1,0:T(8,128)(2,1)}, bf16[13,5,16,128]{3,2,1,0:T(8,128)(2,1)S(1)}, u32[]{:S(2)}, u32[]{:S(2)}) collective-permute-start(bf16[13,5,16,128]{3,2,1,0:T(8,128)(2,1)} %get-tuple-element.98), channel_id=1, source_target_pairs={{0,1},{1,0},{2,3},{3,2},{4,5},{5,4},{6,7},{7,6},{8,9},{9,8},{10,11... | collective-permute-start | bytes 798728 | tf_op jit(solution)/shard_map/cond/branch_0_fun/ppermute | solution.py:35
  462.1 40.8 %collective-permute-start.19 = (bf16[13,5,16,128]{3,2,1,0:T(8,128)(2,1)}, bf16[13,5,16,128]{3,2,1,0:T(8,128)(2,1)S(1)}, u32[]{:S(2)}, u32[]{:S(2)}) collective-permute-start(bf16[13,5,16,128]{3,2,1,0:T(8,128)(2,1)} %get-tuple-element.99), channel_id=1, source_target_pairs={{0,2},{1,3},{2,0},{3,1},{4,6},{5,7},{6,4},{7,5},{8,10},{9,11},{10,... | collective-permute-start | bytes 798728 | tf_op jit(solution)/shard_map/cond/branch_0_fun/ppermute | solution.py:35
  477.7 27.0 %collective-permute-start.20 = (bf16[13,5,16,128]{3,2,1,0:T(8,128)(2,1)}, bf16[13,5,16,128]{3,2,1,0:T(8,128)(2,1)S(1)}, u32[]{:S(2)}, u32[]{:S(2)}) collective-permute-start(bf16[13,5,16,128]{3,2,1,0:T(8,128)(2,1)} %get-tuple-element.100), channel_id=1, source_target_pairs={{0,3},{1,2},{2,1},{3,0},{4,7},{5,6},{6,5},{7,4},{8,11},{9,10},{10,... | collective-permute-start | bytes 798728 | tf_op jit(solution)/shard_map/cond/branch_0_fun/ppermute | solution.py:35
  480.6 24.6 %collective-permute-start.21 = (bf16[13,5,16,128]{3,2,1,0:T(8,128)(2,1)}, bf16[13,5,16,128]{3,2,1,0:T(8,128)(2,1)S(1)}, u32[]{:S(2)}, u32[]{:S(2)}) collective-permute-start(bf16[13,5,16,128]{3,2,1,0:T(8,128)(2,1)} %get-tuple-element.101), channel_id=1, source_target_pairs={{0,4},{1,5},{2,6},{3,7},{4,0},{5,1},{6,2},{7,3},{8,12},{9,13},{10,... | collective-permute-start | bytes 798728 | tf_op jit(solution)/shard_map/cond/branch_0_fun/ppermute | solution.py:35
  489.3 39.3 %collective-permute-start.22 = (bf16[13,5,16,128]{3,2,1,0:T(8,128)(2,1)}, bf16[13,5,16,128]{3,2,1,0:T(8,128)(2,1)S(1)}, u32[]{:S(2)}, u32[]{:S(2)}) collective-permute-start(bf16[13,5,16,128]{3,2,1,0:T(8,128)(2,1)} %get-tuple-element.102), channel_id=1, source_target_pairs={{0,5},{1,4},{2,7},{3,6},{4,1},{5,0},{6,3},{7,2},{8,13},{9,12},{10,... | collective-permute-start | bytes 798728 | tf_op jit(solution)/shard_map/cond/branch_0_fun/ppermute | solution.py:35
  502.8 25.7 %collective-permute-start.23 = (bf16[13,5,16,128]{3,2,1,0:T(8,128)(2,1)}, bf16[13,5,16,128]{3,2,1,0:T(8,128)(2,1)}, u32[]{:S(2)}, u32[]{:S(2)}) collective-permute-start(bf16[13,5,16,128]{3,2,1,0:T(8,128)(2,1)} %get-tuple-element.103), channel_id=1, source_target_pairs={{0,6},{1,7},{2,4},{3,5},{4,2},{5,3},{6,0},{7,1},{8,14},{9,15},{10,... | collective-permute-start | bytes 798728 | tf_op jit(solution)/shard_map/cond/branch_0_fun/ppermute | solution.py:35
  502.9 29.5 %collective-permute-start.24 = (bf16[13,5,16,128]{3,2,1,0:T(8,128)(2,1)}, bf16[13,5,16,128]{3,2,1,0:T(8,128)(2,1)}, u32[]{:S(2)}, u32[]{:S(2)}) collective-permute-start(bf16[13,5,16,128]{3,2,1,0:T(8,128)(2,1)} %get-tuple-element.104), channel_id=1, source_target_pairs={{0,7},{1,6},{2,5},{3,4},{4,3},{5,2},{6,1},{7,0},{8,15},{9,14},{10,... | collective-permute-start | bytes 798728 | tf_op jit(solution)/shard_map/cond/branch_0_fun/ppermute | solution.py:35
  504.7 55.5 %collective-permute-start.47 = (bf16[13,2,16,128]{3,2,1,0:T(8,128)(2,1)}, bf16[13,2,16,128]{3,2,1,0:T(8,128)(2,1)S(1)}, u32[]{:S(2)}, u32[]{:S(2)}) collective-permute-start(bf16[13,2,16,128]{3,2,1,0:T(8,128)(2,1)} %get-tuple-element.127), channel_id=1, source_target_pairs={{0,3},{1,2},{2,1},{3,0},{4,7},{5,6},{6,5},{7,4},{8,11},{9,10},{10,... | collective-permute-start | bytes 319496 | tf_op jit(solution)/shard_map/cond/branch_0_fun/ppermute | solution.py:35
  505.2 54.9 %collective-permute-start.48 = (bf16[13,2,16,128]{3,2,1,0:T(8,128)(2,1)}, bf16[13,2,16,128]{3,2,1,0:T(8,128)(2,1)}, u32[]{:S(2)}, u32[]{:S(2)}) collective-permute-start(bf16[13,2,16,128]{3,2,1,0:T(8,128)(2,1)} %get-tuple-element.128), channel_id=1, source_target_pairs={{0,4},{1,5},{2,6},{3,7},{4,0},{5,1},{6,2},{7,3},{8,12},{9,13},{10,... | collective-permute-start | bytes 319496 | tf_op jit(solution)/shard_map/cond/branch_0_fun/ppermute | solution.py:35
  528.6 31.6 %collective-permute-start.49 = (bf16[13,2,16,128]{3,2,1,0:T(8,128)(2,1)}, bf16[13,2,16,128]{3,2,1,0:T(8,128)(2,1)}, u32[]{:S(2)}, u32[]{:S(2)}) collective-permute-start(bf16[13,2,16,128]{3,2,1,0:T(8,128)(2,1)} %get-tuple-element.129), channel_id=1, source_target_pairs={{0,5},{1,4},{2,7},{3,6},{4,1},{5,0},{6,3},{7,2},{8,13},{9,12},{10,... | collective-permute-start | bytes 319496 | tf_op jit(solution)/shard_map/cond/branch_0_fun/ppermute | solution.py:35
  528.6 31.6 %collective-permute-start.50 = (bf16[13,2,16,128]{3,2,1,0:T(8,128)(2,1)}, bf16[13,2,16,128]{3,2,1,0:T(8,128)(2,1)}, u32[]{:S(2)}, u32[]{:S(2)}) collective-permute-start(bf16[13,2,16,128]{3,2,1,0:T(8,128)(2,1)} %get-tuple-element.130), channel_id=1, source_target_pairs={{0,6},{1,7},{2,4},{3,5},{4,2},{5,3},{6,0},{7,1},{8,14},{9,15},{10,... | collective-permute-start | bytes 319496 | tf_op jit(solution)/shard_map/cond/branch_0_fun/ppermute | solution.py:35
  532.3 27.9 %collective-permute-start.51 = (bf16[13,2,16,128]{3,2,1,0:T(8,128)(2,1)}, bf16[13,2,16,128]{3,2,1,0:T(8,128)(2,1)}, u32[]{:S(2)}, u32[]{:S(2)}) collective-permute-start(bf16[13,2,16,128]{3,2,1,0:T(8,128)(2,1)} %get-tuple-element.131), channel_id=1, source_target_pairs={{0,7},{1,6},{2,5},{3,4},{4,3},{5,2},{6,1},{7,0},{8,15},{9,14},{10,... | collective-permute-start | bytes 319496 | tf_op jit(solution)/shard_map/cond/branch_0_fun/ppermute | solution.py:35
  (60 other events, 2824.8 us)
where the time goes:
time: 599 us; the launch traced here: 598 us
  waiting for transfers between devices  320 us (53%)
  Pallas kernels  132 us (22%)
  starting transfers between devices  104 us (17%)
  blocking collectives  27.7 us (5%)
  local copies, waits for them, and re-layouts  9.51 us (2%)
    ppermute x52, waiting for transfers between devices, swap(): return lax.ppermute(value, axis, [(i, i ^ bit) for i in range(size)])  320 us
    ppermute x52, starting transfers between devices, swap(): return lax.ppermute(value, axis, [(i, i ^ bit) for i in range(size)])  99.1 us
    pallas_call x4, Pallas kernels, outer(): pl.pallas_call(functools.partial(outer_kernel, offsets, slots, tile, n_ba...  43 us
    pallas_call x2, Pallas kernels, inner(): pl.pallas_call(functools.partial(inner_kernel, tile, starts, sizes), out_...  31.6 us
    all_to_all x1, blocking collectives, run(): lax.all_to_all(total, ('row', 'col'), split_axis=0, concat_axis=0, tiled=...  27.7 us
    pallas_call x2, Pallas kernels, contract(): pl.pallas_call(functools.partial(contract_kernel, group, counts, cols), o...  20.1 us
    pallas_call x2, Pallas kernels, pack(): pl.pallas_call(functools.partial(pack_kernel, near, slots, tile, n_basis...  17.8 us
  transfers between devices with their start and end apart: 53, of which 18 were waited for; matrix products, arithmetic and copies ran while one was open for 1% of the time, Pallas kernels for 20%

commit v1 on v0

--- a/solution.py
+++ b/solution.py
@@ -24,11 +24,6 @@
         bits.append(bit)
         bit //= 2
     return bits
-
-
-def gather_bits(size):
-    bits = xor_bits(size)
-    return bits[-1:] + bits[:-1]
 
 
 def swap(value, axis, size, bit):
@@ -122,8 +117,8 @@
     )(me, slot_tile, slot_on, b)
 
 
-def lane_block(n_basis):
-    return min(256, n_basis)
+def lane_block(n_basis, most):
+    return min(most, n_basis)
 
 
 def keep_tiles(mask_ref, first, tile, value_ref, out_ref):
@@ -159,7 +154,7 @@
     out_refs, masked = refs[:-1], refs[-1]
     keep_tiles(mask_ref, 0, tile, b_ref.at[0], masked)
     n_basis = masked.shape[1]
-    width = lane_block(n_basis)
+    width = lane_block(n_basis, 512)
     p = pl.program_id(0)
 
     @pl.loop(0, n_basis // width)
@@ -209,7 +204,7 @@
     out_refs, wide = refs[len(offsets) : -1], refs[-1]
     depth = half_refs[0].shape[1]
     rows = out_refs[0].shape[2]
-    width = lane_block(wide.shape[1])
+    width = lane_block(wide.shape[1], 256)
 
     @pl.loop(0, wide.shape[1] // width)
     def _(j):
@@ -411,14 +406,14 @@
     local_mask = lax.dynamic_slice(b_mask, (me[2], row_index * m_tiles, 0), (1, m_tiles, across))[0]
 
     green, seen = jnp.stack([virt_green, occ_green]), []
-    for bit in gather_bits(col_size):
+    for bit in xor_bits(col_size):
         upper = (col_index & bit) != 0
         axis = 1 + sum(other > bit for other in seen)
         seen.append(bit)
         green = join(green, swap(green, "col", col_size, bit), upper, axis)
     virt_rows, occ_rows = green.reshape(2, -1, n_basis)
 
-    early = max(1, p_count // 8)
+    early = max(1, p_count * 3 // 16)
     strips = pack(b_tensor, 0, early, True, me, slot_tile, slot_on, col_size, tile)
     near = exchange(strips)
     (strips,) = pack(

time: 599 us -> 523 us (0.87)
  waiting for transfers between devices: 320 us -> 235 us
  starting transfers between devices: 104 us -> 119 us
  Pallas kernels: 132 us -> 126 us
    ppermute x52, waiting for transfers between devices: 320 us -> 235 us  [swap(): return lax.ppermute(value, axis, [(i, i ^ bit) for i in range(size)])]
    ppermute x52, starting transfers between devices: 99.1 us -> 112 us  [swap(): return lax.ppermute(value, axis, [(i, i ^ bit) for i in range(size)])]
    pallas_call x2, Pallas kernels: 31.6 us -> 25.5 us  [inner(): pl.pallas_call(functools.partial(inner_kernel, tile, starts, sizes), out_...]
  transfers between devices with their start and end apart: 53 -> 53, of which waited for: 18 -> 19; matrix products, arithmetic and copies ran while one was open for 1% -> 1% of each run, Pallas kernels for 20% -> 22%
where the time goes in v1:
time: 523 us; the launch traced here: 522 us
  waiting for transfers between devices  235 us (45%)
  Pallas kernels  126 us (24%)
  starting transfers between devices  119 us (23%)
  blocking collectives  28.1 us (5%)
  local copies, waits for them, and re-layouts  7.98 us (2%)
    ppermute x52, waiting for transfers between devices, swap(): return lax.ppermute(value, axis, [(i, i ^ bit) for i in range(size)])  235 us
    ppermute x52, starting transfers between devices, swap(): return lax.ppermute(value, axis, [(i, i ^ bit) for i in range(size)])  112 us
    pallas_call x4, Pallas kernels, outer(): pl.pallas_call(functools.partial(outer_kernel, offsets, slots, tile, n_ba...  42.9 us
    all_to_all x1, blocking collectives, run(): lax.all_to_all(total, ('row', 'col'), split_axis=0, concat_axis=0, tiled=...  28.1 us
    pallas_call x2, Pallas kernels, inner(): pl.pallas_call(functools.partial(inner_kernel, tile, starts, sizes), out_...  25.5 us
    pallas_call x2, Pallas kernels, contract(): pl.pallas_call(functools.partial(contract_kernel, group, counts, cols), o...  20.1 us
    pallas_call x2, Pallas kernels, pack(): pl.pallas_call(functools.partial(pack_kernel, near, slots, tile, n_basis...  18.3 us
    pallas_call x1, Pallas kernels, flatten(): pl.pallas_call(functools.partial(flatten_kernel, group, early), out_shape...  11 us
  transfers between devices with their start and end apart: 53, of which 19 were waited for; matrix products, arithmetic and copies ran while one was open for 1% of the time, Pallas kernels for 22%

profile of v1, /device:TPU:1, one launch (start us, length us, event | category | flops | bytes accessed | tf_op | source)
XLA Modules:
  0.0 521.6 jit_solution(14260675248546132868)
XLA Ops:
  2.2 518.8 %conditional.1 = (f32[4,128]{1,0:T(4,128)S(1)}) conditional(s32[]{:T(128)} %bitcast.78, (s32[16]{0:T(128)S(1)}, s32[]{:T(128)}, s32[]{:T(128)}, bf16[32,1024]{1,0:T(8,128)(2,1)}, bf16[32,1024]{1,0:T(8,128)(2,1)}, /*index=5*/s32[8,8]{1,0:T(8,128)}, s32[1,8,8]{2,1,0:T(8,128)}, s32[8,8]{1,0:T(8,128)}, bf16[16,256,1024]{2,1,0:T(8,128)(2,1)}, ...), branch_computations={%region_0.2_spmd, %region_2.4_spmd, %region_4.6_spmd} | conditional | flops 6062094 | bytes 239561984 | solution.py:372
  6.3 6.0 %collective-permute-done = bf16[2,32,1024]{2,1,0:T(8,128)(2,1)S(1)} collective-permute-done((bf16[2,32,1024]{2,1,0:T(8,128)(2,1)S(1)}, bf16[2,32,1024]{2,1,0:T(8,128)(2,1)S(1)}, u32[]{:S(2)}, u32[]{:S(2)}) %collective-permute-start) | collective-permute-done | bytes 131104 | tf_op jit(solution)/shard_map/cond/branch_0_fun/ppermute | solution.py:30
  14.5 5.4 %collective-permute-done.1 = bf16[2,2,32,1024]{3,2,1,0:T(8,128)(2,1)S(1)} collective-permute-done((bf16[2,2,32,1024]{3,2,1,0:T(8,128)(2,1)S(1)}, bf16[2,2,32,1024]{3,2,1,0:T(8,128)(2,1)S(1)}, u32[]{:S(2)}, u32[]{:S(2)}) %collective-permute-start.1) | collective-permute-done | bytes 262176 | tf_op jit(solution)/shard_map/cond/branch_0_fun/ppermute | solution.py:30
  21.0 13.4 %branch_0_fun.21 = bf16[8,13,13,16,128]{4,3,2,1,0:T(8,128)(2,1)} custom-call(s32[3]{0:T(128)S(1)} %get-tuple-element.78.me, s32[13]{0:T(128)S(1)} %bitcast.146, s32[13]{0:T(128)S(1)} %bitcast.161, bf16[16,256,1024]{2,1,0:T(8,128)(2,1)} %get-tuple-element.86.b_ref), custom_call_target="tpu_custom_call" | custom-call | tf_op jit(solution)/shard_map/cond/branch_0_fun/pallas_call | solution.py:107
  34.5 6.3 %all-to-all-start = ((bf16[8,13,13,16,128]{4,3,2,1,0:T(8,128)(2,1)}), bf16[8,13,13,16,128]{4,3,2,1,0:T(8,128)(2,1)}, u32[]{:S(2)}, u32[]{:S(2)}) async-start(bf16[8,13,13,16,128]{4,3,2,1,0:T(8,128)(2,1)} %branch_0_fun.21), calls=%async_computation | async-start | bytes 11075584 | tf_op jit(solution)/shard_map/cond/branch_0_fun/all_to_all | solution.py:422
  43.0 10.4 %collective-permute-done.3 = bf16[256,1024]{1,0:T(8,128)(2,1)S(1)} collective-permute-done((bf16[256,1024]{1,0:T(8,128)(2,1)S(1)}, bf16[256,1024]{1,0:T(8,128)(2,1)S(1)}, u32[]{:S(2)}, u32[]{:S(2)}) %collective-permute-start.3) | collective-permute-done | bytes 524320 | tf_op jit(solution)/shard_map/cond/branch_0_fun/ppermute | solution.py:30
  64.7 16.5 %branch_0_fun.17 = (bf16[5,256,1024]{2,1,0:T(8,128)(2,1)}, bf16[4,256,1024]{2,1,0:T(8,128)(2,1)}, bf16[2,256,1024]{2,1,0:T(8,128)(2,1)}) custom-call(s32[2,8]{1,0:T(2,128)} %dynamic-slice_bitcast_fusion.mask_ref, bf16[16,256,1024]{2,1,0:T(8,128)(2,1)} %get-tuple-element.86.b_ref, bf16[1024,1024]{1,0:T(8,128)(2,1)} %branch_0_fun.14.virt_ref), custom_call_target="tpu_custom_call" | custom-call | tf_op jit(solution)/shard_map/cond/branch_0_fun/pallas_call | solution.py:176
  81.5 4.8 branch_0_fun.20
  89.0 9.0 %branch_0_fun.15.refs_0_ = bf16[5,256,1024]{2,1,0:T(8,128)(2,1)} custom-call(s32[2,8]{1,0:T(2,128)} %dynamic-slice_bitcast_fusion.mask_ref, bf16[16,256,1024]{2,1,0:T(8,128)(2,1)} %get-tuple-element.86.b_ref, bf16[1024,1024]{1,0:T(8,128)(2,1)} %branch_0_fun.14.virt_ref), custom_call_target="tpu_custom_call" | custom-call | tf_op jit(solution)/shard_map/cond/branch_0_fun/pallas_call | solution.py:176
  99.5 6.6 %collective-permute-done.35.refs_1_ = bf16[13,3,16,128]{3,2,1,0:T(8,128)(2,1)S(1)} collective-permute-done((bf16[13,3,16,128]{3,2,1,0:T(8,128)(2,1)}, bf16[13,3,16,128]{3,2,1,0:T(8,128)(2,1)S(1)}, u32[]{:S(2)}, u32[]{:S(2)}) %collective-permute-start.35) | collective-permute-done | bytes 159776 | tf_op jit(solution)/shard_map/cond/branch_0_fun/ppermute | solution.py:30
  108.3 24.4 %collective-permute-done.36.refs_2_ = bf16[13,3,16,128]{3,2,1,0:T(8,128)(2,1)S(1)} collective-permute-done((bf16[13,3,16,128]{3,2,1,0:T(8,128)(2,1)}, bf16[13,3,16,128]{3,2,1,0:T(8,128)(2,1)S(1)}, u32[]{:S(2)}, u32[]{:S(2)}) %collective-permute-start.36) | collective-permute-done | bytes 159776 | tf_op jit(solution)/shard_map/cond/branch_0_fun/ppermute | solution.py:30
  138.6 36.3 %collective-permute-done.38.refs_4_ = bf16[13,3,16,128]{3,2,1,0:T(8,128)(2,1)S(1)} collective-permute-done((bf16[13,3,16,128]{3,2,1,0:T(8,128)(2,1)}, bf16[13,3,16,128]{3,2,1,0:T(8,128)(2,1)S(1)}, u32[]{:S(2)}, u32[]{:S(2)}) %collective-permute-start.38) | collective-permute-done | bytes 159776 | tf_op jit(solution)/shard_map/cond/branch_0_fun/ppermute | solution.py:30
  183.9 7.9 %collective-permute-done.41.refs_7_ = bf16[13,3,16,128]{3,2,1,0:T(8,128)(2,1)} collective-permute-done((bf16[13,3,16,128]{3,2,1,0:T(8,128)(2,1)}, bf16[13,3,16,128]{3,2,1,0:T(8,128)(2,1)}, u32[]{:S(2)}, u32[]{:S(2)}) %collective-permute-start.41) | collective-permute-done | bytes 159776 | tf_op jit(solution)/shard_map/cond/branch_0_fun/ppermute | solution.py:30
  193.2 57.9 %collective-permute-done.42.refs_1_ = bf16[2,256,1024]{2,1,0:T(8,128)(2,1)S(1)} collective-permute-done((bf16[2,256,1024]{2,1,0:T(8,128)(2,1)}, bf16[2,256,1024]{2,1,0:T(8,128)(2,1)S(1)}, u32[]{:S(2)}, u32[]{:S(2)}) %collective-permute-start.42) | collective-permute-done | bytes 1048608 | tf_op jit(solution)/shard_map/cond/branch_0_fun/ppermute | solution.py:30
  251.1 10.9 %collective-permute-start.44 = (bf16[2,256,1024]{2,1,0:T(8,128)(2,1)S(1)}, bf16[2,256,1024]{2,1,0:T(8,128)(2,1)S(1)}, u32[]{:S(2)}, u32[]{:S(2)}) collective-permute-start(bf16[2,256,1024]{2,1,0:T(8,128)(2,1)S(1)} %collective-permute-done.42.refs_1_), channel_id=1, source_target_pairs={{0,8},{8,0},{16,24},{24,16},{1,9},{9,1},{17,25},{25,17},{2,10},{10... | collective-permute-start | bytes 3145736 | tf_op jit(solution)/shard_map/cond/branch_0_fun/ppermute | solution.py:30
  267.8 6.9 %branch_0_fun.24 = (bf16[13,2,16,128]{3,2,1,0:T(8,128)(2,1)}, bf16[13,2,16,128]{3,2,1,0:T(8,128)(2,1)}, bf16[13,2,16,128]{3,2,1,0:T(8,128)(2,1)}, bf16[13,2,16,1...) custom-call(s32[3]{0:T(128)S(1)} %get-tuple-element.78.me, ...), custom_call_target="tpu_custom_call" | custom-call | tf_op jit(solution)/shard_map/cond/branch_0_fun/pallas_call | solution.py:237
  274.8 21.4 %collective-permute-done.25.refs_1_ = bf16[4,256,1024]{2,1,0:T(8,128)(2,1)} collective-permute-done((bf16[4,256,1024]{2,1,0:T(8,128)(2,1)}, bf16[4,256,1024]{2,1,0:T(8,128)(2,1)}, u32[]{:S(2)}, u32[]{:S(2)}) %collective-permute-start.25) | collective-permute-done | bytes 2097184 | tf_op jit(solution)/shard_map/cond/branch_0_fun/ppermute | solution.py:30
  296.1 5.0 collective-permute-start.45
  312.1 10.8 %branch_0_fun.19 = (bf16[13,4,16,128]{3,2,1,0:T(8,128)(2,1)}, bf16[13,4,16,128]{3,2,1,0:T(8,128)(2,1)}, bf16[13,4,16,128]{3,2,1,0:T(8,128)(2,1)}, bf16[13,4,16,1...) custom-call(s32[3]{0:T(128)S(1)} %get-tuple-element.78.me, ...), custom_call_target="tpu_custom_call" | custom-call | tf_op jit(solution)/shard_map/cond/branch_0_fun/pallas_call | solution.py:237
  335.2 12.6 %branch_0_fun.16 = (bf16[13,5,16,128]{3,2,1,0:T(8,128)(2,1)}, bf16[13,5,16,128]{3,2,1,0:T(8,128)(2,1)}, bf16[13,5,16,128]{3,2,1,0:T(8,128)(2,1)}, bf16[13,5,16,1...) custom-call(s32[3]{0:T(128)S(1)} %get-tuple-element.78.me, ...), custom_call_target="tpu_custom_call" | custom-call | tf_op jit(solution)/shard_map/cond/branch_0_fun/pallas_call | solution.py:237
  350.2 5.5 %collective-permute-done.32.refs_21_ = bf16[13,4,16,128]{3,2,1,0:T(8,128)(2,1)S(1)} collective-permute-done((bf16[13,4,16,128]{3,2,1,0:T(8,128)(2,1)}, bf16[13,4,16,128]{3,2,1,0:T(8,128)(2,1)S(1)}, u32[]{:S(2)}, u32[]{:S(2)}) %collective-permute-start.32) | collective-permute-done | bytes 213024 | tf_op jit(solution)/shard_map/cond/branch_0_fun/ppermute | solution.py:30
  357.1 4.7 collective-permute-start.11
  363.4 12.6 %branch_0_fun.18 = (bf16[13,5,16,128]{3,2,1,0:T(8,128)(2,1)}, bf16[13,5,16,128]{3,2,1,0:T(8,128)(2,1)}, bf16[13,5,16,128]{3,2,1,0:T(8,128)(2,1)}, bf16[13,5,16,1...) custom-call(s32[3]{0:T(128)S(1)} %get-tuple-element.78.me, ...), custom_call_target="tpu_custom_call" | custom-call | tf_op jit(solution)/shard_map/cond/branch_0_fun/pallas_call | solution.py:237
  376.0 5.6 %collective-permute-start.12 = (bf16[13,5,16,128]{3,2,1,0:T(8,128)(2,1)S(1)}, bf16[13,5,16,128]{3,2,1,0:T(8,128)(2,1)S(1)}, u32[]{:S(2)}, u32[]{:S(2)}) collective-permute-start(bf16[13,5,16,128]{3,2,1,0:T(8,128)(2,1)S(1)} %copy-done.105), channel_id=1, source_target_pairs={{0,5},{1,4},{2,7},{3,6},{4,1},{5,0},{6,3},{7,2},{8,13},{9,12},{10,... | collective-permute-start | bytes 798728 | tf_op jit(solution)/shard_map/cond/branch_0_fun/ppermute | solution.py:30
  386.3 14.7 %collective-permute-done.12.refs_5_ = bf16[13,5,16,128]{3,2,1,0:T(8,128)(2,1)S(1)} collective-permute-done((bf16[13,5,16,128]{3,2,1,0:T(8,128)(2,1)S(1)}, bf16[13,5,16,128]{3,2,1,0:T(8,128)(2,1)S(1)}, u32[]{:S(2)}, u32[]{:S(2)}) %collective-permute-start.12) | collective-permute-done | bytes 266272 | tf_op jit(solution)/shard_map/cond/branch_0_fun/ppermute | solution.py:30
  405.2 7.6 %collective-permute-start.21 = (bf16[13,5,16,128]{3,2,1,0:T(8,128)(2,1)}, bf16[13,5,16,128]{3,2,1,0:T(8,128)(2,1)S(1)}, u32[]{:S(2)}, u32[]{:S(2)}) collective-permute-start(bf16[13,5,16,128]{3,2,1,0:T(8,128)(2,1)} %get-tuple-element.101), channel_id=1, source_target_pairs={{0,4},{1,5},{2,6},{3,7},{4,0},{5,1},{6,2},{7,3},{8,12},{9,13},{10,... | collective-permute-start | bytes 798728 | tf_op jit(solution)/shard_map/cond/branch_0_fun/ppermute | solution.py:30
  412.9 13.2 %collective-permute-start.22 = (bf16[13,5,16,128]{3,2,1,0:T(8,128)(2,1)}, bf16[13,5,16,128]{3,2,1,0:T(8,128)(2,1)S(1)}, u32[]{:S(2)}, u32[]{:S(2)}) collective-permute-start(bf16[13,5,16,128]{3,2,1,0:T(8,128)(2,1)} %get-tuple-element.102), channel_id=1, source_target_pairs={{0,5},{1,4},{2,7},{3,6},{4,1},{5,0},{6,3},{7,2},{8,13},{9,12},{10,... | collective-permute-start | bytes 798728 | tf_op jit(solution)/shard_map/cond/branch_0_fun/ppermute | solution.py:30
  430.6 20.9 %collective-permute-done.22.refs_13_ = bf16[13,5,16,128]{3,2,1,0:T(8,128)(2,1)S(1)} collective-permute-done((bf16[13,5,16,128]{3,2,1,0:T(8,128)(2,1)}, bf16[13,5,16,128]{3,2,1,0:T(8,128)(2,1)S(1)}, u32[]{:S(2)}, u32[]{:S(2)}) %collective-permute-start.22) | collective-permute-done | bytes 266272 | tf_op jit(solution)/shard_map/cond/branch_0_fun/ppermute | solution.py:30
  459.1 11.0 %branch_0_fun.22.refs_24_.refs_8_ = bf16[128,26624]{1,0:T(8,128)(2,1)} custom-call(s32[3]{0:T(128)S(1)} %get-tuple-element.78.me, bf16[13,3,16,128]{3,2,1,0:T(8,128)(2,1)} %get-tuple-element.115.refs_0_, bf16[13,3,16,128]{3,2,1,0:T(8,128)(2,1)} %copy-done.79, bf16[13,3,16,128]{3,2,1,0:T(8,128)(2,1)} %copy-done.80, bf16[13,3,16,128]{3,2,1,0:T(8,128)(2,1)} %copy-done.81, ...), custom_call_target="tpu_custom_call" | custom-call | tf_op jit(solution)/shard_map/cond/branch_0_fun/pallas_call | solution.py:292
  470.3 12.3 %branch_0_fun.23 = f32[112,128]{1,0:T(8,128)} custom-call(s32[3]{0:T(128)S(1)} %get-tuple-element.78.me, bf16[13,5,16,128]{3,2,1,0:T(8,128)(2,1)} %get-tuple-element.88.refs_0_, bf16[13,5,16,128]{3,2,1,0:T(8,128)(2,1)} %copy-done.34, bf16[13,5,16,128]{3,2,1,0:T(8,128)(2,1)} %copy-done.35, bf16[13,5,16,128]{3,2,1,0:T(8,128)(2,1)} %copy-done.36, ...), custom_call_target="tpu_custom_call" | custom-call | tf_op jit(solution)/shard_map/cond/branch_0_fun/pallas_call | solution.py:336
  484.1 7.8 %branch_0_fun.25 = f32[16,128]{1,0:T(8,128)} custom-call(s32[3]{0:T(128)S(1)} %get-tuple-element.78.me, bf16[13,2,16,128]{3,2,1,0:T(8,128)(2,1)} %get-tuple-element.124.refs_0_, bf16[13,2,16,128]{3,2,1,0:T(8,128)(2,1)} %copy-done.91, bf16[13,2,16,128]{3,2,1,0:T(8,128)(2,1)} %collective-permute-done.46.refs_2_, bf16[13,2,16,128]{3,2,1,0:T(8,128)(2,1)} %copy-done.92, ...), custom_call_target="tpu_custom_call" | custom-call | tf_op jit(solution)/shard_map/cond/branch_0_fun/pallas_call | solution.py:336
  492.6 28.1 %all_to_all.24 = f32[32,4,128]{2,1,0:T(4,128)S(1)} all-to-all(f32[32,4,128]{2,1,0:T(4,128)S(1)} %bitcast.143), channel_id=1, replica_groups=mesh['row'=4,'col'=8] {'row','col'}, dimensions={0} | all-to-all | bytes 131072 | tf_op jit(solution)/shard_map/cond/branch_0_fun/all_to_all | solution.py:455
  (184 shorter events, 103.7 us)
Async XLA Ops:
  34.5 424.7 %all-to-all-start = ((bf16[8,13,13,16,128]{4,3,2,1,0:T(8,128)(2,1)}), bf16[8,13,13,16,128]{4,3,2,1,0:T(8,128)(2,1)}, u32[]{:S(2)}, u32[]{:S(2)}) async-start(bf16[8,13,13,16,128]{4,3,2,1,0:T(8,128)(2,1)} %branch_0_fun.21), calls=%async_computation | async-start | bytes 11075584 | tf_op jit(solution)/shard_map/cond/branch_0_fun/all_to_all | solution.py:422
  81.1 111.9 %collective-permute-start.43 = (bf16[2,256,1024]{2,1,0:T(8,128)(2,1)}, bf16[2,256,1024]{2,1,0:T(8,128)(2,1)}, u32[]{:S(2)}, u32[]{:S(2)}) collective-permute-start(bf16[2,256,1024]{2,1,0:T(8,128)(2,1)} %get-tuple-element.123.refs_0_), channel_id=1, source_target_pairs={{0,8},{8,0},{16,24},{24,16},{1,9},{9,1},{17,25},{25,17},{2,10},{10... | collective-permute-start | bytes 3145736 | tf_op jit(solution)/shard_map/cond/branch_0_fun/ppermute | solution.py:30
  87.8 44.9 %collective-permute-start.36 = (bf16[13,3,16,128]{3,2,1,0:T(8,128)(2,1)}, bf16[13,3,16,128]{3,2,1,0:T(8,128)(2,1)S(1)}, u32[]{:S(2)}, u32[]{:S(2)}) collective-permute-start(bf16[13,3,16,128]{3,2,1,0:T(8,128)(2,1)} %get-tuple-element.117), channel_id=1, source_target_pairs={{0,2},{1,3},{2,0},{3,1},{4,6},{5,7},{6,4},{7,5},{8,10},{9,11},{10,... | collective-permute-start | bytes 479240 | tf_op jit(solution)/shard_map/cond/branch_0_fun/ppermute | solution.py:30
  98.0 166.6 %collective-permute-start.5 = (bf16[5,256,1024]{2,1,0:T(8,128)(2,1)}, bf16[5,256,1024]{2,1,0:T(8,128)(2,1)}, u32[]{:S(2)}, u32[]{:S(2)}) collective-permute-start(bf16[5,256,1024]{2,1,0:T(8,128)(2,1)} %branch_0_fun.15.refs_0_), channel_id=1, source_target_pairs={{0,16},{8,24},{16,0},{24,8},{1,17},{9,25},{17,1},{25,9},{2,18},{10... | collective-permute-start | bytes 7864328 | tf_op jit(solution)/shard_map/cond/branch_0_fun/ppermute | solution.py:30
  99.3 37.8 %collective-permute-start.37 = (bf16[13,3,16,128]{3,2,1,0:T(8,128)(2,1)}, bf16[13,3,16,128]{3,2,1,0:T(8,128)(2,1)S(1)}, u32[]{:S(2)}, u32[]{:S(2)}) collective-permute-start(bf16[13,3,16,128]{3,2,1,0:T(8,128)(2,1)} %get-tuple-element.118), channel_id=1, source_target_pairs={{0,3},{1,2},{2,1},{3,0},{4,7},{5,6},{6,5},{7,4},{8,11},{9,10},{10,... | collective-permute-start | bytes 479240 | tf_op jit(solution)/shard_map/cond/branch_0_fun/ppermute | solution.py:30
  106.1 68.9 %collective-permute-start.38 = (bf16[13,3,16,128]{3,2,1,0:T(8,128)(2,1)}, bf16[13,3,16,128]{3,2,1,0:T(8,128)(2,1)S(1)}, u32[]{:S(2)}, u32[]{:S(2)}) collective-permute-start(bf16[13,3,16,128]{3,2,1,0:T(8,128)(2,1)} %get-tuple-element.119), channel_id=1, source_target_pairs={{0,4},{1,5},{2,6},{3,7},{4,0},{5,1},{6,2},{7,3},{8,12},{9,13},{10,... | collective-permute-start | bytes 479240 | tf_op jit(solution)/shard_map/cond/branch_0_fun/ppermute | solution.py:30
  132.7 48.0 %collective-permute-start.39 = (bf16[13,3,16,128]{3,2,1,0:T(8,128)(2,1)}, bf16[13,3,16,128]{3,2,1,0:T(8,128)(2,1)S(1)}, u32[]{:S(2)}, u32[]{:S(2)}) collective-permute-start(bf16[13,3,16,128]{3,2,1,0:T(8,128)(2,1)} %get-tuple-element.120), channel_id=1, source_target_pairs={{0,5},{1,4},{2,7},{3,6},{4,1},{5,0},{6,3},{7,2},{8,13},{9,12},{10,... | collective-permute-start | bytes 479240 | tf_op jit(solution)/shard_map/cond/branch_0_fun/ppermute | solution.py:30
  137.1 46.0 %collective-permute-start.40 = (bf16[13,3,16,128]{3,2,1,0:T(8,128)(2,1)}, bf16[13,3,16,128]{3,2,1,0:T(8,128)(2,1)S(1)}, u32[]{:S(2)}, u32[]{:S(2)}) collective-permute-start(bf16[13,3,16,128]{3,2,1,0:T(8,128)(2,1)} %get-tuple-element.121), channel_id=1, source_target_pairs={{0,6},{1,7},{2,4},{3,5},{4,2},{5,3},{6,0},{7,1},{8,14},{9,15},{10,... | collective-permute-start | bytes 479240 | tf_op jit(solution)/shard_map/cond/branch_0_fun/ppermute | solution.py:30
  175.0 132.6 %collective-permute-start.15 = (bf16[5,256,1024]{2,1,0:T(8,128)(2,1)S(1)}, bf16[5,256,1024]{2,1,0:T(8,128)(2,1)}, u32[]{:S(2)}, u32[]{:S(2)}) collective-permute-start(bf16[5,256,1024]{2,1,0:T(8,128)(2,1)S(1)} %copy-done), channel_id=1, source_target_pairs={{0,16},{8,24},{16,0},{24,8},{1,17},{9,25},{17,1},{25,9},{2,18},{10... | collective-permute-start | bytes 7864328 | tf_op jit(solution)/shard_map/cond/branch_0_fun/ppermute | solution.py:30
  180.7 81.3 %collective-permute-start.26 = (bf16[4,256,1024]{2,1,0:T(8,128)(2,1)}, bf16[4,256,1024]{2,1,0:T(8,128)(2,1)S(1)}, u32[]{:S(2)}, u32[]{:S(2)}) collective-permute-start(bf16[4,256,1024]{2,1,0:T(8,128)(2,1)} %get-tuple-element.105.refs_0_), channel_id=1, source_target_pairs={{0,8},{8,0},{16,24},{24,16},{1,9},{9,1},{17,25},{25,17},{2,10},{10... | collective-permute-start | bytes 6291464 | tf_op jit(solution)/shard_map/cond/branch_0_fun/ppermute | solution.py:30
  191.7 59.3 %collective-permute-start.42 = (bf16[2,256,1024]{2,1,0:T(8,128)(2,1)}, bf16[2,256,1024]{2,1,0:T(8,128)(2,1)S(1)}, u32[]{:S(2)}, u32[]{:S(2)}) collective-permute-start(bf16[2,256,1024]{2,1,0:T(8,128)(2,1)} %get-tuple-element.123.refs_0_), channel_id=1, source_target_pairs={{0,16},{8,24},{16,0},{24,8},{1,17},{9,25},{17,1},{25,9},{2,18},{10... | collective-permute-start | bytes 3145736 | tf_op jit(solution)/shard_map/cond/branch_0_fun/ppermute | solution.py:30
  193.0 103.1 %collective-permute-start.25 = (bf16[4,256,1024]{2,1,0:T(8,128)(2,1)}, bf16[4,256,1024]{2,1,0:T(8,128)(2,1)}, u32[]{:S(2)}, u32[]{:S(2)}) collective-permute-start(bf16[4,256,1024]{2,1,0:T(8,128)(2,1)} %get-tuple-element.105.refs_0_), channel_id=1, source_target_pairs={{0,16},{8,24},{16,0},{24,8},{1,17},{9,25},{17,1},{25,9},{2,18},{10... | collective-permute-start | bytes 6291464 | tf_op jit(solution)/shard_map/cond/branch_0_fun/ppermute | solution.py:30
  262.0 62.3 %collective-permute-start.6 = (bf16[5,256,1024]{2,1,0:T(8,128)(2,1)}, bf16[5,256,1024]{2,1,0:T(8,128)(2,1)}, u32[]{:S(2)}, u32[]{:S(2)}) collective-permute-start(bf16[5,256,1024]{2,1,0:T(8,128)(2,1)} %branch_0_fun.15.refs_0_), channel_id=1, source_target_pairs={{0,8},{8,0},{16,24},{24,16},{1,9},{9,1},{17,25},{25,17},{2,10},{10... | collective-permute-start | bytes 7864328 | tf_op jit(solution)/shard_map/cond/branch_0_fun/ppermute | solution.py:30
  264.3 61.5 %collective-permute-start.16 = (bf16[5,256,1024]{2,1,0:T(8,128)(2,1)S(1)}, bf16[5,256,1024]{2,1,0:T(8,128)(2,1)}, u32[]{:S(2)}, u32[]{:S(2)}) collective-permute-start(bf16[5,256,1024]{2,1,0:T(8,128)(2,1)S(1)} %copy-done), channel_id=1, source_target_pairs={{0,8},{8,0},{16,24},{24,16},{1,9},{9,1},{17,25},{25,17},{2,10},{10... | collective-permute-start | bytes 7864328 | tf_op jit(solution)/shard_map/cond/branch_0_fun/ppermute | solution.py:30
  264.6 68.6 %collective-permute-start.7 = (bf16[5,256,1024]{2,1,0:T(8,128)(2,1)}, bf16[5,256,1024]{2,1,0:T(8,128)(2,1)}, u32[]{:S(2)}, u32[]{:S(2)}) collective-permute-start(bf16[5,256,1024]{2,1,0:T(8,128)(2,1)} %collective-permute-done.5.refs_1_), channel_id=1, source_target_pairs={{0,8},{8,0},{16,24},{24,16},{1,9},{9,1},{17,25},{25,17},{2,10},{10... | collective-permute-start | bytes 7864328 | tf_op jit(solution)/shard_map/cond/branch_0_fun/ppermute | solution.py:30
  307.5 54.2 %collective-permute-start.17 = (bf16[5,256,1024]{2,1,0:T(8,128)(2,1)}, bf16[5,256,1024]{2,1,0:T(8,128)(2,1)}, u32[]{:S(2)}, u32[]{:S(2)}) collective-permute-start(bf16[5,256,1024]{2,1,0:T(8,128)(2,1)} %collective-permute-done.15.refs_1_), channel_id=1, source_target_pairs={{0,8},{8,0},{16,24},{24,16},{1,9},{9,1},{17,25},{25,17},{2,10},{10... | collective-permute-start | bytes 7864328 | tf_op jit(solution)/shard_map/cond/branch_0_fun/ppermute | solution.py:30
  348.5 33.1 %collective-permute-start.8 = (bf16[13,5,16,128]{3,2,1,0:T(8,128)(2,1)}, bf16[13,5,16,128]{3,2,1,0:T(8,128)(2,1)S(1)}, u32[]{:S(2)}, u32[]{:S(2)}) collective-permute-start(bf16[13,5,16,128]{3,2,1,0:T(8,128)(2,1)} %get-tuple-element.89), channel_id=1, source_target_pairs={{0,1},{1,0},{2,3},{3,2},{4,5},{5,4},{6,7},{7,6},{8,9},{9,8},{10,11... | collective-permute-start | bytes 798728 | tf_op jit(solution)/shard_map/cond/branch_0_fun/ppermute | solution.py:30
  349.9 35.1 %collective-permute-start.9 = (bf16[13,5,16,128]{3,2,1,0:T(8,128)(2,1)}, bf16[13,5,16,128]{3,2,1,0:T(8,128)(2,1)S(1)}, u32[]{:S(2)}, u32[]{:S(2)}) collective-permute-start(bf16[13,5,16,128]{3,2,1,0:T(8,128)(2,1)} %get-tuple-element.90), channel_id=1, source_target_pairs={{0,2},{1,3},{2,0},{3,1},{4,6},{5,7},{6,4},{7,5},{8,10},{9,11},{10,... | collective-permute-start | bytes 798728 | tf_op jit(solution)/shard_map/cond/branch_0_fun/ppermute | solution.py:30
  356.3 29.5 %collective-permute-start.10 = (bf16[13,5,16,128]{3,2,1,0:T(8,128)(2,1)}, bf16[13,5,16,128]{3,2,1,0:T(8,128)(2,1)S(1)}, u32[]{:S(2)}, u32[]{:S(2)}) collective-permute-start(bf16[13,5,16,128]{3,2,1,0:T(8,128)(2,1)} %get-tuple-element.91), channel_id=1, source_target_pairs={{0,3},{1,2},{2,1},{3,0},{4,7},{5,6},{6,5},{7,4},{8,11},{9,10},{10,... | collective-permute-start | bytes 798728 | tf_op jit(solution)/shard_map/cond/branch_0_fun/ppermute | solution.py:30
  357.1 29.2 %collective-permute-start.11 = (bf16[13,5,16,128]{3,2,1,0:T(8,128)(2,1)}, bf16[13,5,16,128]{3,2,1,0:T(8,128)(2,1)S(1)}, u32[]{:S(2)}, u32[]{:S(2)}) collective-permute-start(bf16[13,5,16,128]{3,2,1,0:T(8,128)(2,1)} %get-tuple-element.92), channel_id=1, source_target_pairs={{0,4},{1,5},{2,6},{3,7},{4,0},{5,1},{6,2},{7,3},{8,12},{9,13},{10,... | collective-permute-start | bytes 798728 | tf_op jit(solution)/shard_map/cond/branch_0_fun/ppermute | solution.py:30
  384.9 27.9 %collective-permute-start.14 = (bf16[13,5,16,128]{3,2,1,0:T(8,128)(2,1)S(1)}, bf16[13,5,16,128]{3,2,1,0:T(8,128)(2,1)S(1)}, u32[]{:S(2)}, u32[]{:S(2)}) collective-permute-start(bf16[13,5,16,128]{3,2,1,0:T(8,128)(2,1)S(1)} %copy-done.103), channel_id=1, source_target_pairs={{0,7},{1,6},{2,5},{3,4},{4,3},{5,2},{6,1},{7,0},{8,15},{9,14},{10,... | collective-permute-start | bytes 798728 | tf_op jit(solution)/shard_map/cond/branch_0_fun/ppermute | solution.py:30
  385.9 40.2 %collective-permute-start.18 = (bf16[13,5,16,128]{3,2,1,0:T(8,128)(2,1)}, bf16[13,5,16,128]{3,2,1,0:T(8,128)(2,1)S(1)}, u32[]{:S(2)}, u32[]{:S(2)}) collective-permute-start(bf16[13,5,16,128]{3,2,1,0:T(8,128)(2,1)} %get-tuple-element.98), channel_id=1, source_target_pairs={{0,1},{1,0},{2,3},{3,2},{4,5},{5,4},{6,7},{7,6},{8,9},{9,8},{10,11... | collective-permute-start | bytes 798728 | tf_op jit(solution)/shard_map/cond/branch_0_fun/ppermute | solution.py:30
  386.2 39.8 %collective-permute-start.19 = (bf16[13,5,16,128]{3,2,1,0:T(8,128)(2,1)}, bf16[13,5,16,128]{3,2,1,0:T(8,128)(2,1)S(1)}, u32[]{:S(2)}, u32[]{:S(2)}) collective-permute-start(bf16[13,5,16,128]{3,2,1,0:T(8,128)(2,1)} %get-tuple-element.99), channel_id=1, source_target_pairs={{0,2},{1,3},{2,0},{3,1},{4,6},{5,7},{6,4},{7,5},{8,10},{9,11},{10,... | collective-permute-start | bytes 798728 | tf_op jit(solution)/shard_map/cond/branch_0_fun/ppermute | solution.py:30
  400.9 28.2 %collective-permute-start.20 = (bf16[13,5,16,128]{3,2,1,0:T(8,128)(2,1)}, bf16[13,5,16,128]{3,2,1,0:T(8,128)(2,1)S(1)}, u32[]{:S(2)}, u32[]{:S(2)}) collective-permute-start(bf16[13,5,16,128]{3,2,1,0:T(8,128)(2,1)} %get-tuple-element.100), channel_id=1, source_target_pairs={{0,3},{1,2},{2,1},{3,0},{4,7},{5,6},{6,5},{7,4},{8,11},{9,10},{10,... | collective-permute-start | bytes 798728 | tf_op jit(solution)/shard_map/cond/branch_0_fun/ppermute | solution.py:30
  412.9 38.7 %collective-permute-start.22 = (bf16[13,5,16,128]{3,2,1,0:T(8,128)(2,1)}, bf16[13,5,16,128]{3,2,1,0:T(8,128)(2,1)S(1)}, u32[]{:S(2)}, u32[]{:S(2)}) collective-permute-start(bf16[13,5,16,128]{3,2,1,0:T(8,128)(2,1)} %get-tuple-element.102), channel_id=1, source_target_pairs={{0,5},{1,4},{2,7},{3,6},{4,1},{5,0},{6,3},{7,2},{8,13},{9,12},{10,... | collective-permute-start | bytes 798728 | tf_op jit(solution)/shard_map/cond/branch_0_fun/ppermute | solution.py:30
  426.1 25.5 %collective-permute-start.23 = (bf16[13,5,16,128]{3,2,1,0:T(8,128)(2,1)}, bf16[13,5,16,128]{3,2,1,0:T(8,128)(2,1)}, u32[]{:S(2)}, u32[]{:S(2)}) collective-permute-start(bf16[13,5,16,128]{3,2,1,0:T(8,128)(2,1)} %get-tuple-element.103), channel_id=1, source_target_pairs={{0,6},{1,7},{2,4},{3,5},{4,2},{5,3},{6,0},{7,1},{8,14},{9,15},{10,... | collective-permute-start | bytes 798728 | tf_op jit(solution)/shard_map/cond/branch_0_fun/ppermute | solution.py:30
  426.1 29.5 %collective-permute-start.24 = (bf16[13,5,16,128]{3,2,1,0:T(8,128)(2,1)}, bf16[13,5,16,128]{3,2,1,0:T(8,128)(2,1)}, u32[]{:S(2)}, u32[]{:S(2)}) collective-permute-start(bf16[13,5,16,128]{3,2,1,0:T(8,128)(2,1)} %get-tuple-element.104), channel_id=1, source_target_pairs={{0,7},{1,6},{2,5},{3,4},{4,3},{5,2},{6,1},{7,0},{8,15},{9,14},{10,... | collective-permute-start | bytes 798728 | tf_op jit(solution)/shard_map/cond/branch_0_fun/ppermute | solution.py:30
  429.1 54.3 %collective-permute-start.47 = (bf16[13,2,16,128]{3,2,1,0:T(8,128)(2,1)}, bf16[13,2,16,128]{3,2,1,0:T(8,128)(2,1)S(1)}, u32[]{:S(2)}, u32[]{:S(2)}) collective-permute-start(bf16[13,2,16,128]{3,2,1,0:T(8,128)(2,1)} %get-tuple-element.127), channel_id=1, source_target_pairs={{0,3},{1,2},{2,1},{3,0},{4,7},{5,6},{6,5},{7,4},{8,11},{9,10},{10,... | collective-permute-start | bytes 319496 | tf_op jit(solution)/shard_map/cond/branch_0_fun/ppermute | solution.py:30
  429.9 53.6 %collective-permute-start.48 = (bf16[13,2,16,128]{3,2,1,0:T(8,128)(2,1)}, bf16[13,2,16,128]{3,2,1,0:T(8,128)(2,1)}, u32[]{:S(2)}, u32[]{:S(2)}) collective-permute-start(bf16[13,2,16,128]{3,2,1,0:T(8,128)(2,1)} %get-tuple-element.128), channel_id=1, source_target_pairs={{0,4},{1,5},{2,6},{3,7},{4,0},{5,1},{6,2},{7,3},{8,12},{9,13},{10,... | collective-permute-start | bytes 319496 | tf_op jit(solution)/shard_map/cond/branch_0_fun/ppermute | solution.py:30
  451.5 31.9 %collective-permute-start.49 = (bf16[13,2,16,128]{3,2,1,0:T(8,128)(2,1)}, bf16[13,2,16,128]{3,2,1,0:T(8,128)(2,1)}, u32[]{:S(2)}, u32[]{:S(2)}) collective-permute-start(bf16[13,2,16,128]{3,2,1,0:T(8,128)(2,1)} %get-tuple-element.129), channel_id=1, source_target_pairs={{0,5},{1,4},{2,7},{3,6},{4,1},{5,0},{6,3},{7,2},{8,13},{9,12},{10,... | collective-permute-start | bytes 319496 | tf_op jit(solution)/shard_map/cond/branch_0_fun/ppermute | solution.py:30
  451.6 31.9 %collective-permute-start.50 = (bf16[13,2,16,128]{3,2,1,0:T(8,128)(2,1)}, bf16[13,2,16,128]{3,2,1,0:T(8,128)(2,1)}, u32[]{:S(2)}, u32[]{:S(2)}) collective-permute-start(bf16[13,2,16,128]{3,2,1,0:T(8,128)(2,1)} %get-tuple-element.130), channel_id=1, source_target_pairs={{0,6},{1,7},{2,4},{3,5},{4,2},{5,3},{6,0},{7,1},{8,14},{9,15},{10,... | collective-permute-start | bytes 319496 | tf_op jit(solution)/shard_map/cond/branch_0_fun/ppermute | solution.py:30
  455.6 27.8 %collective-permute-start.51 = (bf16[13,2,16,128]{3,2,1,0:T(8,128)(2,1)}, bf16[13,2,16,128]{3,2,1,0:T(8,128)(2,1)}, u32[]{:S(2)}, u32[]{:S(2)}) collective-permute-start(bf16[13,2,16,128]{3,2,1,0:T(8,128)(2,1)} %get-tuple-element.131), channel_id=1, source_target_pairs={{0,7},{1,6},{2,5},{3,4},{4,3},{5,2},{6,1},{7,0},{8,15},{9,14},{10,... | collective-permute-start | bytes 319496 | tf_op jit(solution)/shard_map/cond/branch_0_fun/ppermute | solution.py:30
  (59 other events, 2474.8 us)

commit v2 on v1

--- a/solution.py
+++ b/solution.py
@@ -312,7 +312,7 @@
     def _():
         out_ref[...] = jnp.zeros_like(out_ref)
 
-    @pl.loop(0, group)
+    @pl.loop(0, group, unroll=1 if group % 2 else 2)
     def _(slot):
         base = 0
         for i, count in enumerate(counts):
@@ -413,7 +413,8 @@
         green = join(green, swap(green, "col", col_size, bit), upper, axis)
     virt_rows, occ_rows = green.reshape(2, -1, n_basis)
 
-    early = max(1, p_count * 3 // 16)
+    crowded = slot_tile.shape[0] * 16 >= m_tiles * across * 14
+    early = max(1, p_count * (4 if crowded else 3) // 16)
     strips = pack(b_tensor, 0, early, True, me, slot_tile, slot_on, col_size, tile)
     near = exchange(strips)
     (strips,) = pack(

time: 523 us -> 523 us (level)
  no operation moved by 1% of the time
where the time goes in v2:
time: 523 us; the launch traced here: 522 us
  waiting for transfers between devices  235 us (45%)
  Pallas kernels  126 us (24%)
  starting transfers between devices  119 us (23%)
  blocking collectives  28.2 us (5%)
  local copies, waits for them, and re-layouts  7.93 us (2%)
    ppermute x52, waiting for transfers between devices, swap(): return lax.ppermute(value, axis, [(i, i ^ bit) for i in range(size)])  235 us
    ppermute x52, starting transfers between devices, swap(): return lax.ppermute(value, axis, [(i, i ^ bit) for i in range(size)])  113 us
    pallas_call x4, Pallas kernels, outer(): pl.pallas_call(functools.partial(outer_kernel, offsets, slots, tile, n_ba...  42.9 us
    all_to_all x1, blocking collectives, run(): lax.all_to_all(total, ('row', 'col'), split_axis=0, concat_axis=0, tiled=...  28.2 us
    pallas_call x2, Pallas kernels, inner(): pl.pallas_call(functools.partial(inner_kernel, tile, starts, sizes), out_...  25.4 us
    pallas_call x2, Pallas kernels, contract(): pl.pallas_call(functools.partial(contract_kernel, group, counts, cols), o...  20.1 us
    pallas_call x2, Pallas kernels, pack(): pl.pallas_call(functools.partial(pack_kernel, near, slots, tile, n_basis...  18.2 us
    pallas_call x1, Pallas kernels, flatten(): pl.pallas_call(functools.partial(flatten_kernel, group, early), out_shape...  11.1 us
  transfers between devices with their start and end apart: 53, of which 19 were waited for; matrix products, arithmetic and copies ran while one was open for 1% of the time, Pallas kernels for 22%

profile of v2, /device:TPU:1, one launch (start us, length us, event | category | flops | bytes accessed | tf_op | source)
XLA Modules:
  0.0 521.6 jit_solution(17127376073189506934)
XLA Ops:
  2.2 518.9 %conditional.1 = (f32[4,128]{1,0:T(4,128)S(1)}) conditional(s32[]{:T(128)} %bitcast.78, (s32[16]{0:T(128)S(1)}, s32[]{:T(128)}, s32[]{:T(128)}, bf16[32,1024]{1,0:T(8,128)(2,1)}, bf16[32,1024]{1,0:T(8,128)(2,1)}, /*index=5*/s32[8,8]{1,0:T(8,128)}, s32[1,8,8]{2,1,0:T(8,128)}, s32[8,8]{1,0:T(8,128)}, bf16[16,256,1024]{2,1,0:T(8,128)(2,1)}, ...), branch_computations={%region_0.2_spmd, %region_2.4_spmd, %region_4.6_spmd} | conditional | flops 6062094 | bytes 238185600 | solution.py:372
  6.3 6.0 %collective-permute-done = bf16[2,32,1024]{2,1,0:T(8,128)(2,1)S(1)} collective-permute-done((bf16[2,32,1024]{2,1,0:T(8,128)(2,1)S(1)}, bf16[2,32,1024]{2,1,0:T(8,128)(2,1)S(1)}, u32[]{:S(2)}, u32[]{:S(2)}) %collective-permute-start) | collective-permute-done | bytes 131104 | tf_op jit(solution)/shard_map/cond/branch_0_fun/ppermute | solution.py:30
  14.5 5.4 %collective-permute-done.1 = bf16[2,2,32,1024]{3,2,1,0:T(8,128)(2,1)S(1)} collective-permute-done((bf16[2,2,32,1024]{3,2,1,0:T(8,128)(2,1)S(1)}, bf16[2,2,32,1024]{3,2,1,0:T(8,128)(2,1)S(1)}, u32[]{:S(2)}, u32[]{:S(2)}) %collective-permute-start.1) | collective-permute-done | bytes 262176 | tf_op jit(solution)/shard_map/cond/branch_0_fun/ppermute | solution.py:30
  21.0 13.4 %branch_0_fun.21 = bf16[8,13,13,16,128]{4,3,2,1,0:T(8,128)(2,1)} custom-call(s32[3]{0:T(128)S(1)} %get-tuple-element.78.me, s32[13]{0:T(128)S(1)} %bitcast.146, s32[13]{0:T(128)S(1)} %bitcast.161, bf16[16,256,1024]{2,1,0:T(8,128)(2,1)} %get-tuple-element.86.b_ref), custom_call_target="tpu_custom_call" | custom-call | tf_op jit(solution)/shard_map/cond/branch_0_fun/pallas_call | solution.py:107
  34.5 6.3 %all-to-all-start = ((bf16[8,13,13,16,128]{4,3,2,1,0:T(8,128)(2,1)}), bf16[8,13,13,16,128]{4,3,2,1,0:T(8,128)(2,1)}, u32[]{:S(2)}, u32[]{:S(2)}) async-start(bf16[8,13,13,16,128]{4,3,2,1,0:T(8,128)(2,1)} %branch_0_fun.21), calls=%async_computation | async-start | bytes 11075584 | tf_op jit(solution)/shard_map/cond/branch_0_fun/all_to_all | solution.py:423
  43.0 10.4 %collective-permute-done.3 = bf16[256,1024]{1,0:T(8,128)(2,1)S(1)} collective-permute-done((bf16[256,1024]{1,0:T(8,128)(2,1)S(1)}, bf16[256,1024]{1,0:T(8,128)(2,1)S(1)}, u32[]{:S(2)}, u32[]{:S(2)}) %collective-permute-start.3) | collective-permute-done | bytes 524320 | tf_op jit(solution)/shard_map/cond/branch_0_fun/ppermute | solution.py:30
  64.7 16.4 %branch_0_fun.17 = (bf16[5,256,1024]{2,1,0:T(8,128)(2,1)}, bf16[4,256,1024]{2,1,0:T(8,128)(2,1)}, bf16[2,256,1024]{2,1,0:T(8,128)(2,1)}) custom-call(s32[2,8]{1,0:T(2,128)} %dynamic-slice_bitcast_fusion.mask_ref, bf16[16,256,1024]{2,1,0:T(8,128)(2,1)} %get-tuple-element.86.b_ref, bf16[1024,1024]{1,0:T(8,128)(2,1)} %branch_0_fun.14.virt_ref), custom_call_target="tpu_custom_call" | custom-call | tf_op jit(solution)/shard_map/cond/branch_0_fun/pallas_call | solution.py:176
  81.5 4.8 branch_0_fun.20
  89.0 9.0 %branch_0_fun.15.refs_0_ = bf16[5,256,1024]{2,1,0:T(8,128)(2,1)} custom-call(s32[2,8]{1,0:T(2,128)} %dynamic-slice_bitcast_fusion.mask_ref, bf16[16,256,1024]{2,1,0:T(8,128)(2,1)} %get-tuple-element.86.b_ref, bf16[1024,1024]{1,0:T(8,128)(2,1)} %branch_0_fun.14.virt_ref), custom_call_target="tpu_custom_call" | custom-call | tf_op jit(solution)/shard_map/cond/branch_0_fun/pallas_call | solution.py:176
  99.5 6.6 %collective-permute-done.35.refs_1_ = bf16[13,3,16,128]{3,2,1,0:T(8,128)(2,1)S(1)} collective-permute-done((bf16[13,3,16,128]{3,2,1,0:T(8,128)(2,1)}, bf16[13,3,16,128]{3,2,1,0:T(8,128)(2,1)S(1)}, u32[]{:S(2)}, u32[]{:S(2)}) %collective-permute-start.35) | collective-permute-done | bytes 159776 | tf_op jit(solution)/shard_map/cond/branch_0_fun/ppermute | solution.py:30
  108.3 24.4 %collective-permute-done.36.refs_2_ = bf16[13,3,16,128]{3,2,1,0:T(8,128)(2,1)S(1)} collective-permute-done((bf16[13,3,16,128]{3,2,1,0:T(8,128)(2,1)}, bf16[13,3,16,128]{3,2,1,0:T(8,128)(2,1)S(1)}, u32[]{:S(2)}, u32[]{:S(2)}) %collective-permute-start.36) | collective-permute-done | bytes 159776 | tf_op jit(solution)/shard_map/cond/branch_0_fun/ppermute | solution.py:30
  138.6 36.2 %collective-permute-done.38.refs_4_ = bf16[13,3,16,128]{3,2,1,0:T(8,128)(2,1)S(1)} collective-permute-done((bf16[13,3,16,128]{3,2,1,0:T(8,128)(2,1)}, bf16[13,3,16,128]{3,2,1,0:T(8,128)(2,1)S(1)}, u32[]{:S(2)}, u32[]{:S(2)}) %collective-permute-start.38) | collective-permute-done | bytes 159776 | tf_op jit(solution)/shard_map/cond/branch_0_fun/ppermute | solution.py:30
  183.8 7.9 %collective-permute-done.41.refs_7_ = bf16[13,3,16,128]{3,2,1,0:T(8,128)(2,1)} collective-permute-done((bf16[13,3,16,128]{3,2,1,0:T(8,128)(2,1)}, bf16[13,3,16,128]{3,2,1,0:T(8,128)(2,1)}, u32[]{:S(2)}, u32[]{:S(2)}) %collective-permute-start.41) | collective-permute-done | bytes 159776 | tf_op jit(solution)/shard_map/cond/branch_0_fun/ppermute | solution.py:30
  193.2 57.7 %collective-permute-done.42.refs_1_ = bf16[2,256,1024]{2,1,0:T(8,128)(2,1)S(1)} collective-permute-done((bf16[2,256,1024]{2,1,0:T(8,128)(2,1)}, bf16[2,256,1024]{2,1,0:T(8,128)(2,1)S(1)}, u32[]{:S(2)}, u32[]{:S(2)}) %collective-permute-start.42) | collective-permute-done | bytes 1048608 | tf_op jit(solution)/shard_map/cond/branch_0_fun/ppermute | solution.py:30
  250.9 11.1 %collective-permute-start.44 = (bf16[2,256,1024]{2,1,0:T(8,128)(2,1)S(1)}, bf16[2,256,1024]{2,1,0:T(8,128)(2,1)S(1)}, u32[]{:S(2)}, u32[]{:S(2)}) collective-permute-start(bf16[2,256,1024]{2,1,0:T(8,128)(2,1)S(1)} %collective-permute-done.42.refs_1_), channel_id=1, source_target_pairs={{0,8},{8,0},{16,24},{24,16},{1,9},{9,1},{17,25},{25,17},{2,10},{10... | collective-permute-start | bytes 3145736 | tf_op jit(solution)/shard_map/cond/branch_0_fun/ppermute | solution.py:30
  267.8 6.9 %branch_0_fun.24 = (bf16[13,2,16,128]{3,2,1,0:T(8,128)(2,1)}, bf16[13,2,16,128]{3,2,1,0:T(8,128)(2,1)}, bf16[13,2,16,128]{3,2,1,0:T(8,128)(2,1)}, bf16[13,2,16,1...) custom-call(s32[3]{0:T(128)S(1)} %get-tuple-element.78.me, ...), custom_call_target="tpu_custom_call" | custom-call | tf_op jit(solution)/shard_map/cond/branch_0_fun/pallas_call | solution.py:237
  274.7 21.2 %collective-permute-done.25.refs_1_ = bf16[4,256,1024]{2,1,0:T(8,128)(2,1)} collective-permute-done((bf16[4,256,1024]{2,1,0:T(8,128)(2,1)}, bf16[4,256,1024]{2,1,0:T(8,128)(2,1)}, u32[]{:S(2)}, u32[]{:S(2)}) %collective-permute-start.25) | collective-permute-done | bytes 2097184 | tf_op jit(solution)/shard_map/cond/branch_0_fun/ppermute | solution.py:30
  295.9 5.2 collective-permute-start.45
  312.1 10.8 %branch_0_fun.19 = (bf16[13,4,16,128]{3,2,1,0:T(8,128)(2,1)}, bf16[13,4,16,128]{3,2,1,0:T(8,128)(2,1)}, bf16[13,4,16,128]{3,2,1,0:T(8,128)(2,1)}, bf16[13,4,16,1...) custom-call(s32[3]{0:T(128)S(1)} %get-tuple-element.78.me, ...), custom_call_target="tpu_custom_call" | custom-call | tf_op jit(solution)/shard_map/cond/branch_0_fun/pallas_call | solution.py:237
  335.2 12.6 %branch_0_fun.16 = (bf16[13,5,16,128]{3,2,1,0:T(8,128)(2,1)}, bf16[13,5,16,128]{3,2,1,0:T(8,128)(2,1)}, bf16[13,5,16,128]{3,2,1,0:T(8,128)(2,1)}, bf16[13,5,16,1...) custom-call(s32[3]{0:T(128)S(1)} %get-tuple-element.78.me, ...), custom_call_target="tpu_custom_call" | custom-call | tf_op jit(solution)/shard_map/cond/branch_0_fun/pallas_call | solution.py:237
  350.2 5.5 %collective-permute-done.32.refs_21_ = bf16[13,4,16,128]{3,2,1,0:T(8,128)(2,1)S(1)} collective-permute-done((bf16[13,4,16,128]{3,2,1,0:T(8,128)(2,1)}, bf16[13,4,16,128]{3,2,1,0:T(8,128)(2,1)S(1)}, u32[]{:S(2)}, u32[]{:S(2)}) %collective-permute-start.32) | collective-permute-done | bytes 213024 | tf_op jit(solution)/shard_map/cond/branch_0_fun/ppermute | solution.py:30
  357.0 4.7 collective-permute-start.11
  363.4 12.6 %branch_0_fun.18 = (bf16[13,5,16,128]{3,2,1,0:T(8,128)(2,1)}, bf16[13,5,16,128]{3,2,1,0:T(8,128)(2,1)}, bf16[13,5,16,128]{3,2,1,0:T(8,128)(2,1)}, bf16[13,5,16,1...) custom-call(s32[3]{0:T(128)S(1)} %get-tuple-element.78.me, ...), custom_call_target="tpu_custom_call" | custom-call | tf_op jit(solution)/shard_map/cond/branch_0_fun/pallas_call | solution.py:237
  376.0 5.6 %collective-permute-start.12 = (bf16[13,5,16,128]{3,2,1,0:T(8,128)(2,1)S(1)}, bf16[13,5,16,128]{3,2,1,0:T(8,128)(2,1)S(1)}, u32[]{:S(2)}, u32[]{:S(2)}) collective-permute-start(bf16[13,5,16,128]{3,2,1,0:T(8,128)(2,1)S(1)} %copy-done.97), channel_id=1, source_target_pairs={{0,5},{1,4},{2,7},{3,6},{4,1},{5,0},{6,3},{7,2},{8,13},{9,12},{10,... | collective-permute-start | bytes 798728 | tf_op jit(solution)/shard_map/cond/branch_0_fun/ppermute | solution.py:30
  386.2 14.7 %collective-permute-done.12.refs_5_ = bf16[13,5,16,128]{3,2,1,0:T(8,128)(2,1)S(1)} collective-permute-done((bf16[13,5,16,128]{3,2,1,0:T(8,128)(2,1)S(1)}, bf16[13,5,16,128]{3,2,1,0:T(8,128)(2,1)S(1)}, u32[]{:S(2)}, u32[]{:S(2)}) %collective-permute-start.12) | collective-permute-done | bytes 266272 | tf_op jit(solution)/shard_map/cond/branch_0_fun/ppermute | solution.py:30
  405.0 7.8 %collective-permute-start.21 = (bf16[13,5,16,128]{3,2,1,0:T(8,128)(2,1)}, bf16[13,5,16,128]{3,2,1,0:T(8,128)(2,1)S(1)}, u32[]{:S(2)}, u32[]{:S(2)}) collective-permute-start(bf16[13,5,16,128]{3,2,1,0:T(8,128)(2,1)} %get-tuple-element.101), channel_id=1, source_target_pairs={{0,4},{1,5},{2,6},{3,7},{4,0},{5,1},{6,2},{7,3},{8,12},{9,13},{10,... | collective-permute-start | bytes 798728 | tf_op jit(solution)/shard_map/cond/branch_0_fun/ppermute | solution.py:30
  412.8 13.2 %collective-permute-start.22 = (bf16[13,5,16,128]{3,2,1,0:T(8,128)(2,1)}, bf16[13,5,16,128]{3,2,1,0:T(8,128)(2,1)S(1)}, u32[]{:S(2)}, u32[]{:S(2)}) collective-permute-start(bf16[13,5,16,128]{3,2,1,0:T(8,128)(2,1)} %get-tuple-element.102), channel_id=1, source_target_pairs={{0,5},{1,4},{2,7},{3,6},{4,1},{5,0},{6,3},{7,2},{8,13},{9,12},{10,... | collective-permute-start | bytes 798728 | tf_op jit(solution)/shard_map/cond/branch_0_fun/ppermute | solution.py:30
  430.6 20.9 %collective-permute-done.22.refs_13_ = bf16[13,5,16,128]{3,2,1,0:T(8,128)(2,1)S(1)} collective-permute-done((bf16[13,5,16,128]{3,2,1,0:T(8,128)(2,1)}, bf16[13,5,16,128]{3,2,1,0:T(8,128)(2,1)S(1)}, u32[]{:S(2)}, u32[]{:S(2)}) %collective-permute-start.22) | collective-permute-done | bytes 266272 | tf_op jit(solution)/shard_map/cond/branch_0_fun/ppermute | solution.py:30
  459.1 11.1 %branch_0_fun.22.refs_24_.refs_8_ = bf16[128,26624]{1,0:T(8,128)(2,1)} custom-call(s32[3]{0:T(128)S(1)} %get-tuple-element.78.me, bf16[13,3,16,128]{3,2,1,0:T(8,128)(2,1)} %get-tuple-element.115.refs_0_, bf16[13,3,16,128]{3,2,1,0:T(8,128)(2,1)} %copy-done.73, bf16[13,3,16,128]{3,2,1,0:T(8,128)(2,1)} %copy-done.74, bf16[13,3,16,128]{3,2,1,0:T(8,128)(2,1)} %copy-done.75, ...), custom_call_target="tpu_custom_call" | custom-call | tf_op jit(solution)/shard_map/cond/branch_0_fun/pallas_call | solution.py:292
  470.3 12.3 %branch_0_fun.23 = f32[112,128]{1,0:T(8,128)} custom-call(s32[3]{0:T(128)S(1)} %get-tuple-element.78.me, bf16[13,5,16,128]{3,2,1,0:T(8,128)(2,1)} %get-tuple-element.88.refs_0_, bf16[13,5,16,128]{3,2,1,0:T(8,128)(2,1)} %copy-done.32, bf16[13,5,16,128]{3,2,1,0:T(8,128)(2,1)} %copy-done.33, bf16[13,5,16,128]{3,2,1,0:T(8,128)(2,1)} %copy-done.34, ...), custom_call_target="tpu_custom_call" | custom-call | tf_op jit(solution)/shard_map/cond/branch_0_fun/pallas_call | solution.py:336
  484.0 7.8 %branch_0_fun.25 = f32[16,128]{1,0:T(8,128)} custom-call(s32[3]{0:T(128)S(1)} %get-tuple-element.78.me, bf16[13,2,16,128]{3,2,1,0:T(8,128)(2,1)} %get-tuple-element.124.refs_0_, bf16[13,2,16,128]{3,2,1,0:T(8,128)(2,1)} %copy-done.83, bf16[13,2,16,128]{3,2,1,0:T(8,128)(2,1)} %collective-permute-done.46.refs_2_, bf16[13,2,16,128]{3,2,1,0:T(8,128)(2,1)} %copy-done.84, ...), custom_call_target="tpu_custom_call" | custom-call | tf_op jit(solution)/shard_map/cond/branch_0_fun/pallas_call | solution.py:336
  492.5 28.2 %all_to_all.24 = f32[32,4,128]{2,1,0:T(4,128)S(1)} all-to-all(f32[32,4,128]{2,1,0:T(4,128)S(1)} %bitcast.143), channel_id=1, replica_groups=mesh['row'=4,'col'=8] {'row','col'}, dimensions={0} | all-to-all | bytes 131072 | tf_op jit(solution)/shard_map/cond/branch_0_fun/all_to_all | solution.py:456
  (184 shorter events, 103.6 us)
Async XLA Ops:
  34.5 424.6 %all-to-all-start = ((bf16[8,13,13,16,128]{4,3,2,1,0:T(8,128)(2,1)}), bf16[8,13,13,16,128]{4,3,2,1,0:T(8,128)(2,1)}, u32[]{:S(2)}, u32[]{:S(2)}) async-start(bf16[8,13,13,16,128]{4,3,2,1,0:T(8,128)(2,1)} %branch_0_fun.21), calls=%async_computation | async-start | bytes 11075584 | tf_op jit(solution)/shard_map/cond/branch_0_fun/all_to_all | solution.py:423
  81.1 111.8 %collective-permute-start.43 = (bf16[2,256,1024]{2,1,0:T(8,128)(2,1)}, bf16[2,256,1024]{2,1,0:T(8,128)(2,1)}, u32[]{:S(2)}, u32[]{:S(2)}) collective-permute-start(bf16[2,256,1024]{2,1,0:T(8,128)(2,1)} %get-tuple-element.123.refs_0_), channel_id=1, source_target_pairs={{0,8},{8,0},{16,24},{24,16},{1,9},{9,1},{17,25},{25,17},{2,10},{10... | collective-permute-start | bytes 3145736 | tf_op jit(solution)/shard_map/cond/branch_0_fun/ppermute | solution.py:30
  87.8 44.8 %collective-permute-start.36 = (bf16[13,3,16,128]{3,2,1,0:T(8,128)(2,1)}, bf16[13,3,16,128]{3,2,1,0:T(8,128)(2,1)S(1)}, u32[]{:S(2)}, u32[]{:S(2)}) collective-permute-start(bf16[13,3,16,128]{3,2,1,0:T(8,128)(2,1)} %get-tuple-element.117), channel_id=1, source_target_pairs={{0,2},{1,3},{2,0},{3,1},{4,6},{5,7},{6,4},{7,5},{8,10},{9,11},{10,... | collective-permute-start | bytes 479240 | tf_op jit(solution)/shard_map/cond/branch_0_fun/ppermute | solution.py:30
  98.0 166.6 %collective-permute-start.5 = (bf16[5,256,1024]{2,1,0:T(8,128)(2,1)}, bf16[5,256,1024]{2,1,0:T(8,128)(2,1)}, u32[]{:S(2)}, u32[]{:S(2)}) collective-permute-start(bf16[5,256,1024]{2,1,0:T(8,128)(2,1)} %branch_0_fun.15.refs_0_), channel_id=1, source_target_pairs={{0,16},{8,24},{16,0},{24,8},{1,17},{9,25},{17,1},{25,9},{2,18},{10... | collective-permute-start | bytes 7864328 | tf_op jit(solution)/shard_map/cond/branch_0_fun/ppermute | solution.py:30
  99.3 37.8 %collective-permute-start.37 = (bf16[13,3,16,128]{3,2,1,0:T(8,128)(2,1)}, bf16[13,3,16,128]{3,2,1,0:T(8,128)(2,1)S(1)}, u32[]{:S(2)}, u32[]{:S(2)}) collective-permute-start(bf16[13,3,16,128]{3,2,1,0:T(8,128)(2,1)} %get-tuple-element.118), channel_id=1, source_target_pairs={{0,3},{1,2},{2,1},{3,0},{4,7},{5,6},{6,5},{7,4},{8,11},{9,10},{10,... | collective-permute-start | bytes 479240 | tf_op jit(solution)/shard_map/cond/branch_0_fun/ppermute | solution.py:30
  106.1 68.7 %collective-permute-start.38 = (bf16[13,3,16,128]{3,2,1,0:T(8,128)(2,1)}, bf16[13,3,16,128]{3,2,1,0:T(8,128)(2,1)S(1)}, u32[]{:S(2)}, u32[]{:S(2)}) collective-permute-start(bf16[13,3,16,128]{3,2,1,0:T(8,128)(2,1)} %get-tuple-element.119), channel_id=1, source_target_pairs={{0,4},{1,5},{2,6},{3,7},{4,0},{5,1},{6,2},{7,3},{8,12},{9,13},{10,... | collective-permute-start | bytes 479240 | tf_op jit(solution)/shard_map/cond/branch_0_fun/ppermute | solution.py:30
  132.7 48.0 %collective-permute-start.39 = (bf16[13,3,16,128]{3,2,1,0:T(8,128)(2,1)}, bf16[13,3,16,128]{3,2,1,0:T(8,128)(2,1)S(1)}, u32[]{:S(2)}, u32[]{:S(2)}) collective-permute-start(bf16[13,3,16,128]{3,2,1,0:T(8,128)(2,1)} %get-tuple-element.120), channel_id=1, source_target_pairs={{0,5},{1,4},{2,7},{3,6},{4,1},{5,0},{6,3},{7,2},{8,13},{9,12},{10,... | collective-permute-start | bytes 479240 | tf_op jit(solution)/shard_map/cond/branch_0_fun/ppermute | solution.py:30
  137.0 46.0 %collective-permute-start.40 = (bf16[13,3,16,128]{3,2,1,0:T(8,128)(2,1)}, bf16[13,3,16,128]{3,2,1,0:T(8,128)(2,1)S(1)}, u32[]{:S(2)}, u32[]{:S(2)}) collective-permute-start(bf16[13,3,16,128]{3,2,1,0:T(8,128)(2,1)} %get-tuple-element.121), channel_id=1, source_target_pairs={{0,6},{1,7},{2,4},{3,5},{4,2},{5,3},{6,0},{7,1},{8,14},{9,15},{10,... | collective-permute-start | bytes 479240 | tf_op jit(solution)/shard_map/cond/branch_0_fun/ppermute | solution.py:30
  174.8 132.7 %collective-permute-start.15 = (bf16[5,256,1024]{2,1,0:T(8,128)(2,1)S(1)}, bf16[5,256,1024]{2,1,0:T(8,128)(2,1)}, u32[]{:S(2)}, u32[]{:S(2)}) collective-permute-start(bf16[5,256,1024]{2,1,0:T(8,128)(2,1)S(1)} %copy-done), channel_id=1, source_target_pairs={{0,16},{8,24},{16,0},{24,8},{1,17},{9,25},{17,1},{25,9},{2,18},{10... | collective-permute-start | bytes 7864328 | tf_op jit(solution)/shard_map/cond/branch_0_fun/ppermute | solution.py:30
  180.7 81.2 %collective-permute-start.26 = (bf16[4,256,1024]{2,1,0:T(8,128)(2,1)}, bf16[4,256,1024]{2,1,0:T(8,128)(2,1)S(1)}, u32[]{:S(2)}, u32[]{:S(2)}) collective-permute-start(bf16[4,256,1024]{2,1,0:T(8,128)(2,1)} %get-tuple-element.105.refs_0_), channel_id=1, source_target_pairs={{0,8},{8,0},{16,24},{24,16},{1,9},{9,1},{17,25},{25,17},{2,10},{10... | collective-permute-start | bytes 6291464 | tf_op jit(solution)/shard_map/cond/branch_0_fun/ppermute | solution.py:30
  191.7 59.1 %collective-permute-start.42 = (bf16[2,256,1024]{2,1,0:T(8,128)(2,1)}, bf16[2,256,1024]{2,1,0:T(8,128)(2,1)S(1)}, u32[]{:S(2)}, u32[]{:S(2)}) collective-permute-start(bf16[2,256,1024]{2,1,0:T(8,128)(2,1)} %get-tuple-element.123.refs_0_), channel_id=1, source_target_pairs={{0,16},{8,24},{16,0},{24,8},{1,17},{9,25},{17,1},{25,9},{2,18},{10... | collective-permute-start | bytes 3145736 | tf_op jit(solution)/shard_map/cond/branch_0_fun/ppermute | solution.py:30
  193.0 102.9 %collective-permute-start.25 = (bf16[4,256,1024]{2,1,0:T(8,128)(2,1)}, bf16[4,256,1024]{2,1,0:T(8,128)(2,1)}, u32[]{:S(2)}, u32[]{:S(2)}) collective-permute-start(bf16[4,256,1024]{2,1,0:T(8,128)(2,1)} %get-tuple-element.105.refs_0_), channel_id=1, source_target_pairs={{0,16},{8,24},{16,0},{24,8},{1,17},{9,25},{17,1},{25,9},{2,18},{10... | collective-permute-start | bytes 6291464 | tf_op jit(solution)/shard_map/cond/branch_0_fun/ppermute | solution.py:30
  261.9 62.3 %collective-permute-start.6 = (bf16[5,256,1024]{2,1,0:T(8,128)(2,1)}, bf16[5,256,1024]{2,1,0:T(8,128)(2,1)}, u32[]{:S(2)}, u32[]{:S(2)}) collective-permute-start(bf16[5,256,1024]{2,1,0:T(8,128)(2,1)} %branch_0_fun.15.refs_0_), channel_id=1, source_target_pairs={{0,8},{8,0},{16,24},{24,16},{1,9},{9,1},{17,25},{25,17},{2,10},{10... | collective-permute-start | bytes 7864328 | tf_op jit(solution)/shard_map/cond/branch_0_fun/ppermute | solution.py:30
  264.2 61.5 %collective-permute-start.16 = (bf16[5,256,1024]{2,1,0:T(8,128)(2,1)S(1)}, bf16[5,256,1024]{2,1,0:T(8,128)(2,1)}, u32[]{:S(2)}, u32[]{:S(2)}) collective-permute-start(bf16[5,256,1024]{2,1,0:T(8,128)(2,1)S(1)} %copy-done), channel_id=1, source_target_pairs={{0,8},{8,0},{16,24},{24,16},{1,9},{9,1},{17,25},{25,17},{2,10},{10... | collective-permute-start | bytes 7864328 | tf_op jit(solution)/shard_map/cond/branch_0_fun/ppermute | solution.py:30
  264.6 68.6 %collective-permute-start.7 = (bf16[5,256,1024]{2,1,0:T(8,128)(2,1)}, bf16[5,256,1024]{2,1,0:T(8,128)(2,1)}, u32[]{:S(2)}, u32[]{:S(2)}) collective-permute-start(bf16[5,256,1024]{2,1,0:T(8,128)(2,1)} %collective-permute-done.5.refs_1_), channel_id=1, source_target_pairs={{0,8},{8,0},{16,24},{24,16},{1,9},{9,1},{17,25},{25,17},{2,10},{10... | collective-permute-start | bytes 7864328 | tf_op jit(solution)/shard_map/cond/branch_0_fun/ppermute | solution.py:30
  307.5 54.2 %collective-permute-start.17 = (bf16[5,256,1024]{2,1,0:T(8,128)(2,1)}, bf16[5,256,1024]{2,1,0:T(8,128)(2,1)}, u32[]{:S(2)}, u32[]{:S(2)}) collective-permute-start(bf16[5,256,1024]{2,1,0:T(8,128)(2,1)} %collective-permute-done.15.refs_1_), channel_id=1, source_target_pairs={{0,8},{8,0},{16,24},{24,16},{1,9},{9,1},{17,25},{25,17},{2,10},{10... | collective-permute-start | bytes 7864328 | tf_op jit(solution)/shard_map/cond/branch_0_fun/ppermute | solution.py:30
  348.6 33.0 %collective-permute-start.8 = (bf16[13,5,16,128]{3,2,1,0:T(8,128)(2,1)}, bf16[13,5,16,128]{3,2,1,0:T(8,128)(2,1)S(1)}, u32[]{:S(2)}, u32[]{:S(2)}) collective-permute-start(bf16[13,5,16,128]{3,2,1,0:T(8,128)(2,1)} %get-tuple-element.89), channel_id=1, source_target_pairs={{0,1},{1,0},{2,3},{3,2},{4,5},{5,4},{6,7},{7,6},{8,9},{9,8},{10,11... | collective-permute-start | bytes 798728 | tf_op jit(solution)/shard_map/cond/branch_0_fun/ppermute | solution.py:30
  349.9 35.0 %collective-permute-start.9 = (bf16[13,5,16,128]{3,2,1,0:T(8,128)(2,1)}, bf16[13,5,16,128]{3,2,1,0:T(8,128)(2,1)S(1)}, u32[]{:S(2)}, u32[]{:S(2)}) collective-permute-start(bf16[13,5,16,128]{3,2,1,0:T(8,128)(2,1)} %get-tuple-element.90), channel_id=1, source_target_pairs={{0,2},{1,3},{2,0},{3,1},{4,6},{5,7},{6,4},{7,5},{8,10},{9,11},{10,... | collective-permute-start | bytes 798728 | tf_op jit(solution)/shard_map/cond/branch_0_fun/ppermute | solution.py:30
  356.3 29.6 %collective-permute-start.10 = (bf16[13,5,16,128]{3,2,1,0:T(8,128)(2,1)}, bf16[13,5,16,128]{3,2,1,0:T(8,128)(2,1)S(1)}, u32[]{:S(2)}, u32[]{:S(2)}) collective-permute-start(bf16[13,5,16,128]{3,2,1,0:T(8,128)(2,1)} %get-tuple-element.91), channel_id=1, source_target_pairs={{0,3},{1,2},{2,1},{3,0},{4,7},{5,6},{6,5},{7,4},{8,11},{9,10},{10,... | collective-permute-start | bytes 798728 | tf_op jit(solution)/shard_map/cond/branch_0_fun/ppermute | solution.py:30
  357.0 29.2 %collective-permute-start.11 = (bf16[13,5,16,128]{3,2,1,0:T(8,128)(2,1)}, bf16[13,5,16,128]{3,2,1,0:T(8,128)(2,1)S(1)}, u32[]{:S(2)}, u32[]{:S(2)}) collective-permute-start(bf16[13,5,16,128]{3,2,1,0:T(8,128)(2,1)} %get-tuple-element.92), channel_id=1, source_target_pairs={{0,4},{1,5},{2,6},{3,7},{4,0},{5,1},{6,2},{7,3},{8,12},{9,13},{10,... | collective-permute-start | bytes 798728 | tf_op jit(solution)/shard_map/cond/branch_0_fun/ppermute | solution.py:30
  384.9 27.9 %collective-permute-start.14 = (bf16[13,5,16,128]{3,2,1,0:T(8,128)(2,1)S(1)}, bf16[13,5,16,128]{3,2,1,0:T(8,128)(2,1)S(1)}, u32[]{:S(2)}, u32[]{:S(2)}) collective-permute-start(bf16[13,5,16,128]{3,2,1,0:T(8,128)(2,1)S(1)} %copy-done.95), channel_id=1, source_target_pairs={{0,7},{1,6},{2,5},{3,4},{4,3},{5,2},{6,1},{7,0},{8,15},{9,14},{10,... | collective-permute-start | bytes 798728 | tf_op jit(solution)/shard_map/cond/branch_0_fun/ppermute | solution.py:30
  385.9 40.1 %collective-permute-start.18 = (bf16[13,5,16,128]{3,2,1,0:T(8,128)(2,1)}, bf16[13,5,16,128]{3,2,1,0:T(8,128)(2,1)S(1)}, u32[]{:S(2)}, u32[]{:S(2)}) collective-permute-start(bf16[13,5,16,128]{3,2,1,0:T(8,128)(2,1)} %get-tuple-element.98), channel_id=1, source_target_pairs={{0,1},{1,0},{2,3},{3,2},{4,5},{5,4},{6,7},{7,6},{8,9},{9,8},{10,11... | collective-permute-start | bytes 798728 | tf_op jit(solution)/shard_map/cond/branch_0_fun/ppermute | solution.py:30
  386.2 39.8 %collective-permute-start.19 = (bf16[13,5,16,128]{3,2,1,0:T(8,128)(2,1)}, bf16[13,5,16,128]{3,2,1,0:T(8,128)(2,1)S(1)}, u32[]{:S(2)}, u32[]{:S(2)}) collective-permute-start(bf16[13,5,16,128]{3,2,1,0:T(8,128)(2,1)} %get-tuple-element.99), channel_id=1, source_target_pairs={{0,2},{1,3},{2,0},{3,1},{4,6},{5,7},{6,4},{7,5},{8,10},{9,11},{10,... | collective-permute-start | bytes 798728 | tf_op jit(solution)/shard_map/cond/branch_0_fun/ppermute | solution.py:30
  400.9 28.1 %collective-permute-start.20 = (bf16[13,5,16,128]{3,2,1,0:T(8,128)(2,1)}, bf16[13,5,16,128]{3,2,1,0:T(8,128)(2,1)S(1)}, u32[]{:S(2)}, u32[]{:S(2)}) collective-permute-start(bf16[13,5,16,128]{3,2,1,0:T(8,128)(2,1)} %get-tuple-element.100), channel_id=1, source_target_pairs={{0,3},{1,2},{2,1},{3,0},{4,7},{5,6},{6,5},{7,4},{8,11},{9,10},{10,... | collective-permute-start | bytes 798728 | tf_op jit(solution)/shard_map/cond/branch_0_fun/ppermute | solution.py:30
  412.8 38.7 %collective-permute-start.22 = (bf16[13,5,16,128]{3,2,1,0:T(8,128)(2,1)}, bf16[13,5,16,128]{3,2,1,0:T(8,128)(2,1)S(1)}, u32[]{:S(2)}, u32[]{:S(2)}) collective-permute-start(bf16[13,5,16,128]{3,2,1,0:T(8,128)(2,1)} %get-tuple-element.102), channel_id=1, source_target_pairs={{0,5},{1,4},{2,7},{3,6},{4,1},{5,0},{6,3},{7,2},{8,13},{9,12},{10,... | collective-permute-start | bytes 798728 | tf_op jit(solution)/shard_map/cond/branch_0_fun/ppermute | solution.py:30
  426.0 25.5 %collective-permute-start.23 = (bf16[13,5,16,128]{3,2,1,0:T(8,128)(2,1)}, bf16[13,5,16,128]{3,2,1,0:T(8,128)(2,1)}, u32[]{:S(2)}, u32[]{:S(2)}) collective-permute-start(bf16[13,5,16,128]{3,2,1,0:T(8,128)(2,1)} %get-tuple-element.103), channel_id=1, source_target_pairs={{0,6},{1,7},{2,4},{3,5},{4,2},{5,3},{6,0},{7,1},{8,14},{9,15},{10,... | collective-permute-start | bytes 798728 | tf_op jit(solution)/shard_map/cond/branch_0_fun/ppermute | solution.py:30
  426.1 29.4 %collective-permute-start.24 = (bf16[13,5,16,128]{3,2,1,0:T(8,128)(2,1)}, bf16[13,5,16,128]{3,2,1,0:T(8,128)(2,1)}, u32[]{:S(2)}, u32[]{:S(2)}) collective-permute-start(bf16[13,5,16,128]{3,2,1,0:T(8,128)(2,1)} %get-tuple-element.104), channel_id=1, source_target_pairs={{0,7},{1,6},{2,5},{3,4},{4,3},{5,2},{6,1},{7,0},{8,15},{9,14},{10,... | collective-permute-start | bytes 798728 | tf_op jit(solution)/shard_map/cond/branch_0_fun/ppermute | solution.py:30
  429.0 54.4 %collective-permute-start.47 = (bf16[13,2,16,128]{3,2,1,0:T(8,128)(2,1)}, bf16[13,2,16,128]{3,2,1,0:T(8,128)(2,1)S(1)}, u32[]{:S(2)}, u32[]{:S(2)}) collective-permute-start(bf16[13,2,16,128]{3,2,1,0:T(8,128)(2,1)} %get-tuple-element.127), channel_id=1, source_target_pairs={{0,3},{1,2},{2,1},{3,0},{4,7},{5,6},{6,5},{7,4},{8,11},{9,10},{10,... | collective-permute-start | bytes 319496 | tf_op jit(solution)/shard_map/cond/branch_0_fun/ppermute | solution.py:30
  429.8 53.6 %collective-permute-start.48 = (bf16[13,2,16,128]{3,2,1,0:T(8,128)(2,1)}, bf16[13,2,16,128]{3,2,1,0:T(8,128)(2,1)}, u32[]{:S(2)}, u32[]{:S(2)}) collective-permute-start(bf16[13,2,16,128]{3,2,1,0:T(8,128)(2,1)} %get-tuple-element.128), channel_id=1, source_target_pairs={{0,4},{1,5},{2,6},{3,7},{4,0},{5,1},{6,2},{7,3},{8,12},{9,13},{10,... | collective-permute-start | bytes 319496 | tf_op jit(solution)/shard_map/cond/branch_0_fun/ppermute | solution.py:30
  451.5 31.9 %collective-permute-start.49 = (bf16[13,2,16,128]{3,2,1,0:T(8,128)(2,1)}, bf16[13,2,16,128]{3,2,1,0:T(8,128)(2,1)}, u32[]{:S(2)}, u32[]{:S(2)}) collective-permute-start(bf16[13,2,16,128]{3,2,1,0:T(8,128)(2,1)} %get-tuple-element.129), channel_id=1, source_target_pairs={{0,5},{1,4},{2,7},{3,6},{4,1},{5,0},{6,3},{7,2},{8,13},{9,12},{10,... | collective-permute-start | bytes 319496 | tf_op jit(solution)/shard_map/cond/branch_0_fun/ppermute | solution.py:30
  451.5 31.9 %collective-permute-start.50 = (bf16[13,2,16,128]{3,2,1,0:T(8,128)(2,1)}, bf16[13,2,16,128]{3,2,1,0:T(8,128)(2,1)}, u32[]{:S(2)}, u32[]{:S(2)}) collective-permute-start(bf16[13,2,16,128]{3,2,1,0:T(8,128)(2,1)} %get-tuple-element.130), channel_id=1, source_target_pairs={{0,6},{1,7},{2,4},{3,5},{4,2},{5,3},{6,0},{7,1},{8,14},{9,15},{10,... | collective-permute-start | bytes 319496 | tf_op jit(solution)/shard_map/cond/branch_0_fun/ppermute | solution.py:30
  455.5 28.0 %collective-permute-start.51 = (bf16[13,2,16,128]{3,2,1,0:T(8,128)(2,1)}, bf16[13,2,16,128]{3,2,1,0:T(8,128)(2,1)}, u32[]{:S(2)}, u32[]{:S(2)}) collective-permute-start(bf16[13,2,16,128]{3,2,1,0:T(8,128)(2,1)} %get-tuple-element.131), channel_id=1, source_target_pairs={{0,7},{1,6},{2,5},{3,4},{4,3},{5,2},{6,1},{7,0},{8,15},{9,14},{10,... | collective-permute-start | bytes 319496 | tf_op jit(solution)/shard_map/cond/branch_0_fun/ppermute | solution.py:30
  (59 other events, 2475.7 us)
